TPU v7x, 256 devices: a whole 4x4x8 slice. The times are simulated.
256 devices in a mesh: row: 8 (over z), col: 32 (over x, y, core).
Axes of the slice: x: 4, y: 4, z: 8, core: 2. Of those that a mesh axis runs over, the one named last changes fastest.
Arguments:
- latitude: bfloat16 [16384, 256], P(('row', 'col')), may hold values from -4 to 4
- longitude: bfloat16 [16384, 512], P(('row', 'col')), may hold values from -4 to 4
- weight: bfloat16 [16384], P(('row', 'col')), may hold values from 0.29882812 to 3
- harmonic_index: int32 [2, 24576], P(None, 'col'), may hold values from 0 to 511, as said below
Outputs:
- coefficients: float32 [512, 24576], P(None, 'col')
- residual: float32 [16384, 24576], P('row', 'col')
Inputs may be any that keep to these rules, and one draw needn't show every extreme that they name: The pairs (harmonic_index[0, j], harmonic_index[1, j]) are distinct over all 24576 columns; row 0 is below 256, and harmonic_index[1, j] // 2 never exceeds harmonic_index[0, j].
All inputs are finite; a program needn't handle non-finite values.
Results may differ from a plain program's by a relative error of at most 0.0003.
Values may be sent and summed in bfloat16 or wider, within the bound.
No kernel may reach another device: no remote copies, remote signals or barrier semaphores. Data moves between devices by JAX's collectives and lax.ppermute only.
A program may use at most 128 MiB of HBM per device.

v0:
```python
import math

import jax
import jax.numpy as jnp
from jax import lax
from jax.sharding import PartitionSpec as P

PANEL = 256


def in_one_piece(arrays, axis, dim, along):
    widths = [math.prod(a.shape[along:]) for a in arrays]
    both = jnp.concatenate(
        [a.reshape(*a.shape[:along], w) for a, w in zip(arrays, widths)], axis=along
    )
    result = lax.all_gather(both, axis, axis=dim, tiled=True)
    tiles = jnp.split(result, [sum(widths[:k]) for k in range(1, len(widths))], axis=along)
    return tuple(
        (b.reshape(*result.shape[:along], *a.shape[along:]) for a, b in zip(arrays, tiles))
    )


def picked(array, axis, root):
    return lax.dynamic_index_in_dim(lax.all_gather(array, axis), root, 0, keepdims=False)


def synthesize(latitude, longitude, weight, column_index):
    degree_hot = (
        column_index[0][None, :] == jnp.arange(latitude.shape[1], dtype=jnp.int32)[:, None]
    ).astype(jnp.bfloat16)
    order_hot = (
        column_index[1][None, :] == jnp.arange(longitude.shape[1], dtype=jnp.int32)[:, None]
    ).astype(jnp.bfloat16)
    picked_degree = jnp.dot(latitude, degree_hot, preferred_element_type=jnp.float32)
    picked_order = jnp.dot(longitude, order_hot, preferred_element_type=jnp.float32)
    return weight.astype(jnp.float32)[:, None] * picked_degree * picked_order


def orthonormal(panel_cols, gram_sum):
    lower_factor = jnp.linalg.cholesky(gram_sum)
    return lax.linalg.triangular_solve(lower_factor, panel_cols.T, left_side=True, lower=True)


def remove_span(design, basis_t, top_rows):
    return design - jnp.dot(
        basis_t.T, top_rows, precision=lax.Precision.HIGHEST, preferred_element_type=jnp.float32
    )


def shards(latitude, longitude, weight, harmonic_index):
    tables = in_one_piece((latitude, longitude, weight), "col", 0, 1)
    lead_index = picked(harmonic_index[:, : 2 * PANEL], "col", 0)
    lead_cols = synthesize(tables[0], tables[1], tables[2], lead_index)
    design = synthesize(tables[0], tables[1], tables[2], harmonic_index)
    local_gram = jnp.dot(
        lead_cols.T, lead_cols, precision=lax.Precision.HIGHEST, preferred_element_type=jnp.float32
    )
    gram_sum = lax.psum(local_gram, "row")
    basis_t = orthonormal(lead_cols, gram_sum)
    local_rows = jnp.dot(
        basis_t, design, precision=lax.Precision.HIGHEST, preferred_element_type=jnp.float32
    )
    coefficients = lax.psum(local_rows, "row")
    residual = remove_span(design, basis_t, coefficients)
    return (coefficients, residual)


def solution(mesh):
    return jax.shard_map(
        shards,
        mesh=mesh,
        in_specs=(
            P(("row", "col"), None),
            P(("row", "col"), None),
            P(("row", "col")),
            P(None, "col"),
        ),
        out_specs=(P(None, "col"), P("row", "col")),
        check_vma=False,
    )
```

profile of v0, /device:TPU:2, one launch (start us, length us, event | category | flops | bytes accessed | tf_op | source)
XLA Modules:
  0.0 433.0 jit_solution(3629395771598168058)
XLA Ops:
  8.0 1.5 pad_maximum_fusion.3
  10.2 24.6 %all-gather.1 = s32[32,2,512]{2,1,0:T(2,128)S(1)} all-gather(s32[1,2,512]{2,1,0:T(2,128)S(1)} %slice_bitcast_fusion.8), channel_id=2, replica_groups=mesh['row'=8,'col'=32] {'col'}, dimensions={0}, use_global_device_ids=true | all-gather | bytes 135168 | tf_op jit(solution)/shard_map/all_gather | solution.py:24
  35.6 28.7 %all-gather.4.cloned.1.call-done = bf16[2048,769]{1,0:T(8,128)(2,1)} async-done(((bf16[64,769]{1,0:T(8,128)(2,1)}), bf16[2048,769]{1,0:T(8,128)(2,1)}) %all-gather.4.cloned.1.call-update) | async-done | bytes 3149840 | tf_op jit(solution)/shard_map/all_gather | solution.py:16
  64.3 1.4 convert_reduce_fusion
  65.7 2.0 fusion.20
  69.0 1.9 copy-done
  70.9 8.0 %fusion.49 = f32[512,512]{0,1:T(8,128)} fusion(f32[2048,512]{1,0:T(8,128)S(1)} %multiply_multiply_fusion.1), kind=kOutput, calls=%fused_computation.94 | convolution fusion | flops 6442450944 | bytes 5242880 | tf_op jit(solution)/shard_map/dot_general | solution.py:55
  79.3 2.4 fusion.18
  81.7 4.7 %multiply_multiply_fusion = f32[2048,768]{1,0:T(8,128)} fusion(f32[2048,768]{1,0:T(8,128)S(1)} %fusion.18, f32[2048]{0:T(1024)S(1)} %convert_reduce_fusion, bf16[2048,769]{1,0:T(8,128)(2,1)S(1)} %copy-done.3, s32[768]{0:T(1024)S(1)} %get-tuple-element.10), kind=kOutput, calls=%fused_computation.2 | convolution fusion | flops 1614151680 | bytes 14692352 | tf_op jit(solution)/shard_map/dot_general | solution.py:35
  86.4 68.5 %all-reduce.4.cloned.1.call-done = f32[512,512]{0,1:T(8,128)} async-done(((f32[512,512]{0,1:T(8,128)}), f32[512,512]{0,1:T(8,128)}) %all-reduce.4.cloned.1.call-update) | async-done | bytes 1048592 | tf_op jit(solution)/shard_map/psum | solution.py:58
  154.9 1.6 copy.14
  156.4 1.4 fusion.17
  157.9 11.7 %cholesky.104 = f32[128,128]{1,0:T(8,128)S(1)} custom-call(f32[128,128]{1,0:T(8,128)S(1)} %cholesky.266), custom_call_target="Cholesky" | custom-call | tf_op jit(solution)/shard_map/jit(cholesky)/cholesky | solution.py:40
  169.6 9.8 %custom-call.30 = f32[1,128,128]{1,2,0:T(8,128)S(1)} custom-call(f32[1,128,128]{2,1,0:T(8,128)S(1)} %get-tuple-element.33), custom_call_target="InvertDiagBlocksLowerTriangular" | custom-call | tf_op jit(solution)/shard_map/jit(cholesky)/cholesky | solution.py:40
  180.3 12.2 %cholesky.217 = f32[128,128]{1,0:T(8,128)S(1)} custom-call(f32[128,128]{1,0:T(8,128)S(1)} %cholesky.270), custom_call_target="Cholesky" | custom-call | tf_op jit(solution)/shard_map/jit(cholesky)/cholesky | solution.py:40
  192.4 9.8 %custom-call.31 = f32[1,128,128]{1,2,0:T(8,128)S(1)} custom-call(f32[1,128,128]{2,1,0:T(8,128)S(1)} %get-tuple-element.30), custom_call_target="InvertDiagBlocksLowerTriangular" | custom-call | tf_op jit(solution)/shard_map/jit(cholesky)/cholesky | solution.py:40
  202.9 11.7 %cholesky.238 = f32[128,128]{1,0:T(8,128)S(1)} custom-call(f32[128,128]{1,0:T(8,128)S(1)} %cholesky.275), custom_call_target="Cholesky" | custom-call | tf_op jit(solution)/shard_map/jit(cholesky)/cholesky | solution.py:40
  215.3 9.8 %custom-call.32 = f32[1,128,128]{1,2,0:T(8,128)S(1)} custom-call(f32[1,128,128]{2,1,0:T(8,128)S(1)} %get-tuple-element.27), custom_call_target="InvertDiagBlocksLowerTriangular" | custom-call | tf_op jit(solution)/shard_map/jit(cholesky)/cholesky | solution.py:40
  225.7 11.9 %cholesky.255 = f32[128,128]{1,0:T(8,128)S(1)} custom-call(f32[128,128]{1,0:T(8,128)S(1)} %convolution_subtract_fusion.5), custom_call_target="Cholesky" | custom-call | tf_op jit(solution)/shard_map/jit(cholesky)/cholesky | solution.py:40
  241.7 10.3 %while.1 = (s32[]{:T(128)}, f32[512,512]{1,0:T(8,128)S(1)}, s32[4,2]{0,1:T(2,128)S(1)}, f32[4,128,128]{2,1,0:T(8,128)}, s32[]{:T(128)}) while((s32[]{:T(128)}, f32[512,512]{1,0:T(8,128)S(1)}, s32[4,2]{0,1:T(2,128)S(1)}, f32[4,128,128]{2,1,0:T(8,128)}, s32[]{:T(128)}) %tuple.33), condition=%wide.while_cond, body=%wide.while_body.sunk | while | flops 2 | bytes 132205 | solution.py:41
  242.3 2.0 bitcast_dynamic-update-slice_fusion.2
  244.9 2.0 bitcast_dynamic-update-slice_fusion.2
  247.5 2.0 bitcast_dynamic-update-slice_fusion.2
  250.1 2.0 bitcast_dynamic-update-slice_fusion.2
  252.0 40.2 %custom-call.33 = f32[4,128,128]{1,2,0:T(8,128)S(1)} custom-call(f32[4,128,128]{2,1,0:T(8,128)} %get-tuple-element.9), custom_call_target="InvertDiagBlocksLowerTriangular" | custom-call | tf_op jit(solution)/shard_map/triangular_solve | solution.py:41
  292.2 2.4 fusion.15
  294.7 3.0 convolution_subtract_fusion.2
  298.8 3.5 convolution_subtract_fusion.1
  303.5 6.6 %fusion.6 = f32[128,2048]{0,1:T(8,128)S(1)} fusion(f32[128,2048]{1,0:T(8,128)S(1)} %fusion.35, f32[128,2048]{1,0:T(8,128)S(1)} %fusion.37, f32[128,2048]{1,0:T(8,128)S(1)} %fusion.15, f32[512,2048]{0,1:T(8,128)S(1)} %bitcast.61, f32[512,512]{1,0:T(8,128)} %copy-done.6), kind=kOutput, calls=%fused_computation.12 | convolution fusion | flops 1209794560 | bytes 5439488 | tf_op jit(solution)/shard_map/triangular_solve | solution.py:41
  312.2 11.6 %fusion.9 = f32[512,768]{1,0:T(8,128)} fusion(f32[2048,768]{1,0:T(8,128)S(1)} %bitcast.63, f32[128,2048]{1,0:T(8,128)S(1)} %fusion.34, f32[128,2048]{1,0:T(8,128)S(1)} %fusion.35, f32[128,2048]{1,0:T(8,128)S(1)} %fusion.37, f32[128,2048]{1,0:T(8,128)S(1)} %fusion.15), kind=kOutput, calls=%fused_computation.15 | convolution fusion | flops 9666822144 | bytes 12058624 | tf_op jit(solution)/shard_map/dot_general | solution.py:60
  323.8 77.3 %all-reduce.6.cloned.1.call-done = f32[512,768]{1,0:T(8,128)} async-done(((f32[512,768]{1,0:T(8,128)}), f32[512,768]{1,0:T(8,128)}) %all-reduce.6.cloned.1.call-update) | async-done | bytes 1572880 | tf_op jit(solution)/shard_map/psum | solution.py:63
  401.0 23.9 %convolution_subtract_fusion = f32[2048,768]{1,0:T(8,128)} fusion(f32[2048,768]{1,0:T(8,128)} %multiply_multiply_fusion, f32[512,768]{1,0:T(8,128)} %all-reduce.6.cloned.1.call-done, f32[128,2048]{1,0:T(8,128)} %copy-done.5, f32[128,2048]{1,0:T(8,128)S(1)} %fusion.35, f32[128,2048]{1,0:T(8,128)S(1)} %fusion.37, f32[128,2048]{1,0:T(8,128)S(1)} %fusion.15), kind=kOutput, calls=%fused_computation.5 | convolution fusion | flops 9668395008 | bytes 18350080 | tf_op jit(solution)/shard_map/dot_general | solution.py:45
  (62 shorter events, 16.0 us)
Async XLA Ops:
  7.2 57.1 %all-gather.4.cloned.1.call-start = ((), (), s32[]{:S(2)}) async-start(), calls=%async_computation | async-start | bytes 3784704 | tf_op jit(solution)/shard_map/all_gather | solution.py:16
  9.5 145.4 %all-reduce.4.cloned.1.call-start = ((), (), s32[]{:S(2)}) async-start(), calls=%async_computation.1 | async-start | bytes 2097152 | tf_op jit(solution)/shard_map/psum | solution.py:58
  64.3 3.4 copy-start.2
  69.0 1.9 copy-start
  79.0 322.0 %all-reduce.6.cloned.1.call-start = ((), (), s32[]{:S(2)}) async-start(), calls=%async_computation.2 | async-start | bytes 3145728 | tf_op jit(solution)/shard_map/psum | solution.py:63
  79.3 2.4 copy-start.3
  252.0 46.8 %copy-start.6 = (f32[512,512]{1,0:T(8,128)}, f32[512,512]{1,0:T(8,128)S(1)}, u32[]{:S(2)}) copy-start(f32[512,512]{1,0:T(8,128)S(1)} %get-tuple-element.92) | copy-start | bytes 3145732
  292.2 6.6 %copy-start.1 = (f32[2048,512]{1,0:T(8,128)S(1)}, f32[2048,512]{1,0:T(8,128)}, u32[]{:S(2)}) copy-start(f32[2048,512]{1,0:T(8,128)} %copy-done) | copy-start | bytes 12582916
  298.8 13.4 %slice-start = ((s8[6291456]{0:T(1024)(128)(4,1)}), s8[4194304]{0:T(1024)(128)(4,1)S(1)}, s32[]{:S(2)}) async-start(s8[6291456]{0:T(1024)(128)(4,1)} %bitcast.62), calls=%async_computation.3 | async-start | bytes 8388608
  303.4 8.7 %slice-start.1 = ((s8[6291456]{0:T(1024)(128)(4,1)}), s8[2097152]{0:T(1024)(128)(4,1)S(1)}, s32[]{:S(2)}) async-start(s8[6291456]{0:T(1024)(128)(4,1)} %bitcast.62), calls=%async_computation.4 | async-start | bytes 4194304
  311.2 1.0 copy-start.5
  401.0 23.9 %copy-start.4 = (f32[512,768]{1,0:T(8,128)S(1)}, f32[512,768]{1,0:T(8,128)}, u32[]{:S(2)}) copy-start(f32[512,768]{1,0:T(8,128)} %all-reduce.6.cloned.1.call-done) | copy-start | bytes 4718596
Sparse Core Ops, SparseCore 0:
  11.1 53.1 all-gather.3
  79.1 75.7 all-reduce.3
  323.9 77.1 all-reduce.5
where the time goes:
time: 441 us; the launch traced here: 433 us
  waiting for transfers between devices  174 us (39%)
  other arithmetic  124 us (28%)
  matrix products  74.6 us (17%)
  blocking collectives  24.6 us (6%)
  local copies, waits for them, and re-layouts  18.3 us (4%)
  between operations  17.1 us (4%)
    another operation x14, other arithmetic, orthonormal(): lower_factor = jnp.linalg.cholesky(gram_sum)  79 us
    psum x1, waiting for transfers between devices, shards(): coefficients = lax.psum(local_rows, 'row')  77.3 us
    psum x1, waiting for transfers between devices, shards(): gram_sum = lax.psum(local_gram, 'row')  68.5 us
    another operation x3, other arithmetic, orthonormal(): lax.linalg.triangular_solve(lower_factor, panel_cols.T, left_side=True, l...  40.3 us
    all_gather x1, waiting for transfers between devices, in_one_piece(): result = lax.all_gather(both, axis, axis=dim, tiled=True)  28.7 us
    all_gather x1, blocking collectives, picked(): lax.all_gather(array, axis)  24.6 us
    dot_general x1, matrix products, remove_span(): jnp.dot(basis_t.T, top_rows, precision=lax.Precision.HIGHEST, preferred_e...  23.9 us
    another operation x7, matrix products, orthonormal(): lax.linalg.triangular_solve(lower_factor, panel_cols.T, left_side=True, l...  18.9 us
  transfers between devices with their start and end apart: 3, of which 3 were waited for; matrix products, arithmetic and copies ran while one was open for 2% of the time, Pallas kernels for 0%

commit v1 on v0

v1 whole, which is shorter than its diff:
```python
import functools

import jax
import jax.numpy as jnp
from jax import lax
from jax.experimental import pallas as pl
from jax.experimental.pallas import tpu as pltpu
from jax.sharding import Mesh, PartitionSpec as P

F32 = jnp.float32
BF16 = jnp.bfloat16
NP = 512
NDEG = 256
NORD = 512
TAB = NDEG + NORD
WIDE = TAB + 128
NB = 128
GROUP = 8
HIGHEST = lax.Precision.HIGHEST
VMEM_LIMIT = 28 * 1024 * 1024
SMALL_VMEM = 16 * 1024 * 1024


def dot(a, b, dims=((1,), (0,)), precision=None):
    return lax.dot_general(a, b, (dims, ((), ())), precision=precision, preferred_element_type=F32)


def in_hbm(*arrays):
    return tuple(pltpu.with_memory_space_constraint(x, pltpu.HBM) for x in arrays)


def split(x):
    high = x.astype(BF16)
    return high, (x - high.astype(F32)).astype(BF16)


def pack_kernel(lat_ref, lon_ref, weight_ref, lead_ref, out_ref, flip):
    flip[...] = jnp.zeros_like(flip)
    flip[0:1, 0:64] = weight_ref[...].astype(F32)
    lead = lead_ref[...]
    degree, order = lead[0:1, :], lead[1:2, :]
    half = order >> 1
    for base, row in ((1, degree), (9, half), (17, order - 2 * half)):
        row = row.astype(F32)
        for k in range(NP // 64):
            flip[base + k : base + k + 1, 0:64] = row[:, 64 * k : 64 * (k + 1)]
    tail = flip[...].T[0:64, :].astype(BF16)
    lat, lon = lat_ref[...], lon_ref[...]
    for p in range(out_ref.shape[0]):
        out_ref[p, :, 0:NDEG] = lat
        out_ref[p, :, NDEG:TAB] = lon
        out_ref[p, :, TAB:WIDE] = tail


def pack(latitude, longitude, weight, lead, count):
    epochs = latitude.shape[0]
    return pl.pallas_call(
        pack_kernel,
        out_shape=jax.ShapeDtypeStruct((count, epochs, WIDE), BF16),
        scratch_shapes=[pltpu.VMEM((128, 128), F32)],
        compiler_params=pltpu.CompilerParams(vmem_limit_bytes=SMALL_VMEM),
        name="pack",
    )(*in_hbm(latitude, longitude), weight.reshape(1, -1), lead)


def onehot_kernel(index_ref, deg_ref, order_ref):
    for ref, row in ((deg_ref, 0), (order_ref, 1)):
        wanted = index_ref[row : row + 1, :]
        ref[...] = (lax.broadcasted_iota(jnp.int32, ref.shape, 0) == wanted).astype(BF16)


def onehots(index):
    cols = index.shape[1]
    return pl.pallas_call(
        onehot_kernel,
        out_shape=[jax.ShapeDtypeStruct((NDEG, cols), BF16), jax.ShapeDtypeStruct((NORD, cols), BF16)],
        compiler_params=pltpu.CompilerParams(vmem_limit_bytes=SMALL_VMEM),
        cost_estimate=pl.CostEstimate(flops=TAB * cols, bytes_accessed=2 * TAB * cols, transcendentals=0),
        name="onehots",
    )(index)


def moments_kernel(second, sub, mine_ref, *refs):
    if second:
        table_ref, deg, order, pdeg, pord, cross_in, slice_in = refs[:7]
        cross_ref, slices_ref, design_ref, high_ref, low_ref, total = refs[10:]
    else:
        head_ref, table_ref, deg, order = refs[:4]
        cross_ref, total, design_ref, high_ref, low_ref, pdeg, pord = refs[4:]

    @pl.when(pl.program_id(0) == 0)
    def _():
        if second:
            cross_ref[...] = cross_in[...]
            total[...] = slice_in[...]
            return
        cross_ref[...] = jnp.zeros_like(cross_ref)
        total[...] = jnp.zeros_like(total)
        head = head_ref[0].astype(F32)
        lanes = lax.broadcasted_iota(jnp.int32, (64, NDEG), 1).astype(F32)
        wide = lax.broadcasted_iota(jnp.int32, (64, NORD), 1).astype(F32)
        for k in range(NP // 64):
            d = head[:, 1 + k : 2 + k]
            o = head[:, 9 + k : 10 + k] * 2.0 + head[:, 17 + k : 18 + k]
            pdeg[64 * k : 64 * (k + 1), :] = (d == lanes).astype(BF16)
            pord[64 * k : 64 * (k + 1), :] = (o == wide).astype(BF16)

    part = total.shape[0]
    at = pl.ds(pl.multiple_of(mine_ref[0] * part, part), part)
    last = ((1,), (1,))

    def synthesize(k):
        rows = slice(k * sub, (k + 1) * sub)
        block = slice(k * sub // 64, (k + 1) * sub // 64)

        def columns(lo, hi):
            return table_ref[block, :, lo:hi].reshape(sub, hi - lo)

        lat, lon = columns(0, NDEG), columns(NDEG, TAB)
        weight = columns(TAB, WIDE).astype(F32)[:, 0:1]
        high, low = split(weight * dot(lat, pdeg[...], last) * dot(lon, pord[...], last))
        own = split(weight * dot(lat, pdeg[at, :], last) * dot(lon, pord[at, :], last))
        high_ref[0, rows, :], low_ref[0, rows, :] = high, low
        design = weight * dot(lat, deg[...]) * dot(lon, order[...])
        design_ref[0, rows, :] = design
        return high, low, own, split(design)

    def accumulate(high, low, own, design):
        lhs = jnp.concatenate([high.T, high.T, low.T], axis=1)
        cross_ref[...] += dot(lhs, jnp.concatenate([design[0], design[1], design[0]], axis=0))
        lhs = jnp.concatenate([own[0].T, own[0].T, own[1].T], axis=1)
        total[...] += dot(lhs, jnp.concatenate([high, low, high], axis=0))

    count = high_ref.shape[1] // sub
    ready = synthesize(0)
    for k in range(count):
        following = synthesize(k + 1) if k + 1 < count else None
        accumulate(*ready)
        ready = following
    if second:
        for k in range(slices_ref.shape[0]):
            slices_ref[k] = total[...]


def moments(table, deg, order, mine, part, rows_of, prior=None, rows=512, sub=256):
    epochs, cols = 64 * table.shape[0], deg.shape[1]
    steps = epochs // rows
    second = prior is not None
    half = 1 if second else 0
    whole = lambda i, s: (0, 0)
    along = lambda i, s: (half, i, 0)
    table_spec = pl.BlockSpec((rows // 64, 64, WIDE), lambda i, s: (i, 0, 0))
    fixed = [pl.BlockSpec(x.shape, whole) for x in (deg, order)]
    pdeg_spec, pord_spec = pl.BlockSpec((NP, NDEG), whole), pl.BlockSpec((NP, NORD), whole)
    cross_spec, slice_spec = pl.BlockSpec((NP, cols), whole), pl.BlockSpec((part, NP), whole)
    big_specs = [
        pl.BlockSpec((1, rows, cols), along),
        pl.BlockSpec((1, rows, NP), along),
        pl.BlockSpec((1, rows, NP), along),
    ]
    big_shapes = [
        pltpu.HBM((2, epochs, cols), F32),
        pltpu.HBM((2, epochs, NP), BF16),
        pltpu.HBM((2, epochs, NP), BF16),
    ]
    cross_shape = (pltpu.HBM if second else jax.ShapeDtypeStruct)((NP, cols), F32)
    if second:
        cross, total, design, high, low, pdeg, pord = prior
        args = (table, deg, order, pdeg, pord, cross, total, *in_hbm(design, high, low))
        in_specs = [table_spec, *fixed, pdeg_spec, pord_spec, cross_spec, slice_spec]
        in_specs += [pl.BlockSpec(memory_space=pl.ANY)] * 3
        out_specs = [cross_spec, pl.BlockSpec((rows_of, part, NP), lambda i, s: (0, 0, 0)), *big_specs]
        out_shape = [cross_shape, jax.ShapeDtypeStruct((rows_of, part, NP), F32), *big_shapes]
        scratch = [pltpu.VMEM((part, NP), F32)]
        aliases = {8: 2, 9: 3, 10: 4}
    else:
        args = (table, table, deg, order)
        in_specs = [pl.BlockSpec((1, 64, 128), lambda i, s: (0, 0, TAB // 128)), table_spec, *fixed]
        out_specs = [cross_spec, slice_spec, *big_specs, pdeg_spec, pord_spec]
        out_shape = [
            cross_shape,
            jax.ShapeDtypeStruct((part, NP), F32),
            *big_shapes,
            jax.ShapeDtypeStruct((NP, NDEG), BF16),
            jax.ShapeDtypeStruct((NP, NORD), BF16),
        ]
        scratch, aliases = [], {}
    return pl.pallas_call(
        functools.partial(moments_kernel, second, sub),
        grid_spec=pltpu.PrefetchScalarGridSpec(
            num_scalar_prefetch=1, grid=(steps,), in_specs=in_specs, out_specs=out_specs, scratch_shapes=scratch
        ),
        out_shape=out_shape,
        input_output_aliases=aliases,
        compiler_params=pltpu.CompilerParams(vmem_limit_bytes=VMEM_LIMIT),
        cost_estimate=pl.CostEstimate(
            flops=2 * epochs * (NP + cols) * TAB + 6 * epochs * cols * NP,
            bytes_accessed=epochs * (2 * WIDE + 4 * cols + 4 * NP),
            transcendentals=0,
        ),
        name="moments_second" if second else "moments_first",
    )(mine, *args)


def invert_block(s_ref, t_ref, x_ref):
    full = (GROUP, NB)
    for g in range(NB // GROUP):
        lo = GROUP * g
        rows = [jnp.broadcast_to(s_ref[lo + i : lo + i + 1, :], full) for i in range(GROUP)]
        extra = [jnp.broadcast_to(t_ref[lo + i : lo + i + 1, :], full) for i in range(GROUP)]
        s = [[jnp.broadcast_to(rows[i][:, lo + j : lo + j + 1], full) for j in range(i + 1)] for i in range(GROUP)]
        inv = [None] * GROUP
        mult = [[None] * GROUP for _ in range(GROUP)]
        for p in range(GROUP):
            inv[p] = 1.0 / s[p][p]
            for i in range(p + 1, GROUP):
                mult[i][p] = s[i][p] * inv[p]
            for i in range(p + 1, GROUP):
                for j in range(p + 1, i + 1):
                    s[i][j] = s[i][j] - mult[i][p] * s[j][p]
            for i in range(p + 1, GROUP):
                rows[i] = rows[i] - mult[i][p] * rows[p]
                extra[i] = extra[i] - mult[i][p] * extra[p]
        for i in range(GROUP):
            x_ref[lo + i : lo + i + 1, :] = (lax.rsqrt(s[i][i]) * extra[i])[0:1, :]
        if g == NB // GROUP - 1:
            break
        y = [r * v for r, v in zip(rows, inv)]
        z = [e * v for e, v in zip(extra, inv)]
        for i in range(GROUP - 1, 0, -1):
            for m in range(i):
                y[m] = y[m] - mult[i][m] * y[i]
                z[m] = z[m] - mult[i][m] * z[i]
        for h in range(g + 1, NB // GROUP):
            at = slice(GROUP * h, GROUP * (h + 1))
            tile = s_ref[at, :]
            other = t_ref[at, :]
            for m in range(GROUP):
                col = jnp.broadcast_to(tile[:, lo + m : lo + m + 1], full)
                if m == 0:
                    da, db = col * y[m], col * z[m]
                else:
                    da, db = da + col * y[m], db + col * z[m]
            s_ref[at, :] = tile - da
            t_ref[at, :] = other - db


def factor_kernel(gram_ref, out_ref, a_ref, s_ref, t_ref, x_ref):
    cores, planes, part = gram_ref.shape[:3]
    for p in range(planes):
        for c in range(cores):
            at = part * (cores * p + c)
            a_ref[at : at + part, :] = gram_ref[c, p]
    out_ref[...] = jnp.zeros_like(out_ref)
    unit = (
        lax.broadcasted_iota(jnp.int32, (NB, NB), 0) == lax.broadcasted_iota(jnp.int32, (NB, NB), 1)
    ).astype(F32)
    count = NP // NB

    @pl.loop(0, count)
    def _(k):
        for i in range(count):

            @pl.when(k == i)
            def _():
                at = slice(NB * i, NB * (i + 1))
                s_ref[...] = a_ref[at, at]

        t_ref[...] = unit
        invert_block(s_ref, t_ref, x_ref)
        for i in range(count):

            @pl.when(k == i)
            def _():
                at = slice(NB * i, NB * (i + 1))
                x = x_ref[...]
                out_ref[at, at] = x
                if i > 0:
                    done = slice(0, NB * i)
                    out_ref[at, done] = dot(x, out_ref[at, done], precision=HIGHEST)
                if i < count - 1:
                    rest = slice(NB * (i + 1), NP)
                    upper = dot(x, a_ref[at, rest], precision=HIGHEST)
                    a_ref[rest, rest] -= dot(upper, upper, ((0,), (0,)), HIGHEST)
                    done = slice(0, NB * (i + 1))
                    out_ref[rest, done] -= dot(upper, out_ref[at, done], ((0,), (0,)), HIGHEST)


def inverse_factor(gram):
    return pl.pallas_call(
        factor_kernel,
        out_shape=jax.ShapeDtypeStruct((NP, NP), F32),
        scratch_shapes=[pltpu.VMEM((NP, NP), F32)] + [pltpu.VMEM((NB, NB), F32)] * 3,
        compiler_params=pltpu.CompilerParams(vmem_limit_bytes=SMALL_VMEM),
        cost_estimate=pl.CostEstimate(flops=300_000_000, bytes_accessed=2 * 4 * NP * NP, transcendentals=0),
        name="inverse_factor",
    )(gram)


def basis_kernel(inv_ref, high_ref, low_ref, qhigh_ref, qlow_ref):
    xhigh, xlow = split(inv_ref[...])
    last = ((1,), (1,))
    high = high_ref[0]
    basis = dot(high, xhigh, last) + dot(high, xlow, last) + dot(low_ref[0], xhigh, last)
    qhigh_ref[0], qlow_ref[0] = split(basis)


def basis_of(inv, high, low, rows=512):
    halves, epochs = high.shape[:2]
    spec = pl.BlockSpec((1, rows, NP), lambda h, i: (h, i, 0))
    return pl.pallas_call(
        basis_kernel,
        grid=(halves, epochs // rows),
        in_specs=[pl.BlockSpec((NP, NP), lambda h, i: (0, 0)), spec, spec],
        out_specs=[spec, spec],
        out_shape=[pltpu.HBM(high.shape, BF16)] * 2,
        compiler_params=pltpu.CompilerParams(vmem_limit_bytes=SMALL_VMEM),
        cost_estimate=pl.CostEstimate(
            flops=12 * epochs * NP * NP, bytes_accessed=16 * epochs * NP, transcendentals=0
        ),
        name="basis_of",
    )(inv, *in_hbm(high, low))


def project_kernel(core_ref, inv_ref, cross_ref, high_ref, low_ref, design_ref, coef_ref, rest_ref, chigh, clow):
    @pl.when((pl.program_id(0) == 0) & (pl.program_id(1) == 0))
    def _():
        coef = dot(inv_ref[...], cross_ref[...], precision=HIGHEST)
        coef_ref[...] = coef
        chigh[...], clow[...] = split(coef)

    high = high_ref[0]
    rest = design_ref[0] - (dot(high, chigh[...]) + dot(high, clow[...]) + dot(low_ref[0], chigh[...]))
    rest_ref[...] = rest.reshape(rest_ref.shape)


def project(core, inv, cross, high, low, design, rows=256):
    halves, epochs, cols = design.shape
    whole = lambda h, i, s: (0, 0)
    along = lambda h, i, s: (h, i, 0)
    tall = rows // 64
    return pl.pallas_call(
        project_kernel,
        grid_spec=pltpu.PrefetchScalarGridSpec(
            num_scalar_prefetch=1,
            grid=(halves, epochs // rows),
            in_specs=[
                pl.BlockSpec((NP, NP), whole),
                pl.BlockSpec((NP, cols), whole),
                pl.BlockSpec((1, rows, NP), along),
                pl.BlockSpec((1, rows, NP), along),
                pl.BlockSpec((1, rows, cols), along),
            ],
            out_specs=[
                pl.BlockSpec((NP, cols), whole),
                pl.BlockSpec((tall, 1, 64, cols), lambda h, i, s: (i, (s[0] + h) % 2, 0, 0)),
            ],
            scratch_shapes=[pltpu.VMEM((NP, cols), BF16), pltpu.VMEM((NP, cols), BF16)],
        ),
        out_shape=[
            jax.ShapeDtypeStruct((NP, cols), F32),
            jax.ShapeDtypeStruct((epochs // 64, halves, 64, cols), F32),
        ],
        compiler_params=pltpu.CompilerParams(vmem_limit_bytes=SMALL_VMEM),
        cost_estimate=pl.CostEstimate(
            flops=12 * epochs * cols * NP, bytes_accessed=2 * epochs * (8 * cols + 4 * NP), transcendentals=0
        ),
        name="project",
    )(core, inv, *in_hbm(cross, high, low, design))


def copies(x, count):
    return jnp.broadcast_to(x[None], (count, *x.shape))


def shards(latitude, longitude, weight, harmonic_index):
    plane, cores, nrow = ("x", "y"), lax.axis_size("core"), lax.axis_size("row")
    places = lax.axis_size("x") * lax.axis_size("y")
    core = lax.axis_index("core")
    mine = (lax.axis_index(plane) * cores + core).reshape(1)
    lead = lax.all_gather(harmonic_index[:, :NP], "core")[0]
    packed = pack(latitude, longitude, weight, lead, places)
    deg, order = onehots(harmonic_index)
    own = lax.all_to_all(packed, plane, 0, 0)
    other = lax.ppermute(own, "core", [(k, (k + 1) % cores) for k in range(cores)])
    part = NP // (places * cores)
    first = moments(own, deg, order, mine, part, nrow)
    cross, slices, design, high, low = moments(other, deg, order, mine, part, nrow, first)
    cross = lax.psum(cross, "row")
    summed = lax.all_to_all(slices, "row", 0, 0).sum(0)
    near = lax.all_to_all(copies(summed, places), plane, 0, 0)
    gram = lax.all_to_all(copies(near, cores), "core", 0, 0)
    inv = inverse_factor(gram)
    qhigh, qlow = basis_of(inv, high, low)
    coefficients, rest = project(core.reshape(1), inv, cross, qhigh, qlow, design)
    return coefficients, rest.reshape(-1, rest.shape[-1])


def solution(mesh):
    sizes = dict(mesh.shape)
    side = int(round((sizes["col"] // 2) ** 0.5))
    fine = Mesh(
        mesh.devices.reshape(sizes["row"], side, sizes["col"] // (2 * side), 2), ("row", "x", "y", "core")
    )
    col = ("x", "y", "core")
    every = ("row", *col)
    return jax.shard_map(
        shards,
        mesh=fine,
        in_specs=(P(every, None), P(every, None), P(every), P(None, col)),
        out_specs=(P(None, col), P("row", col)),
        check_vma=False,
    )
```

time: 441 us -> 161 us (0.37); the launches traced: 433 us -> 160 us
  waiting for transfers between devices: 174 us -> 10.4 us
  other arithmetic: 124 us -> 0.02 us
  matrix products: 74.6 us -> 0 us
  Pallas kernels: 0 us -> 59.5 us
  blocking collectives: 24.6 us -> 74.7 us
  local copies, waits for them, and re-layouts: 18.3 us -> 1.53 us
    psum x2 -> x1, waiting for transfers between devices: 146 us -> 10.4 us  [shards(): cross = lax.psum(cross, 'row')]
    another operation x17 -> x0, other arithmetic: 119 us -> none  [the longest x14 79 us: orthonormal(): lower_factor = jnp.linalg.cholesky(gram_sum)]
    all_to_all x0 -> x4, blocking collectives: none -> 72.9 us  [the longest x1 31.3 us: shards(): own = lax.all_to_all(packed, plane, 0, 0)]
    pallas_call x0 -> x7, Pallas kernels: none -> 59.5 us  [the longest x1 21.3 us: inverse_factor(): pl.pallas_call(factor_kernel, out_shape=jax.ShapeDtypeStruct((NP, NP), F3...]
    dot_general x7 -> x0, matrix products: 53.9 us -> none  [the longest x1 23.9 us: remove_span(): jnp.dot(basis_t.T, top_rows, precision=lax.Precision.HIGHEST, preferred_e...]
    all_gather x1 -> x0, waiting for transfers between devices: 28.7 us -> none  [in_one_piece(): result = lax.all_gather(both, axis, axis=dim, tiled=True)]
    all_gather x1, blocking collectives: 24.6 us -> 1.78 us  [shards(): lead = lax.all_gather(harmonic_index[:, :NP], 'core')[0]]
    another operation x13 -> x0, matrix products: 20.7 us -> none  [the longest x7 18.9 us: orthonormal(): lax.linalg.triangular_solve(lower_factor, panel_cols.T, left_side=True, l...]
  transfers between devices with their start and end apart: 3 -> 2, of which waited for: 3 -> 1; matrix products, arithmetic and copies ran while one was open for 2% -> 0% of each run, Pallas kernels for 0% -> 22%
where the time goes in v1:
time: 161 us; the launch traced here: 160 us
  blocking collectives  74.7 us (46%)
  Pallas kernels  59.5 us (37%)
  between operations  14.1 us (9%)
  waiting for transfers between devices  10.4 us (6%)
    all_to_all x1, blocking collectives, shards(): own = lax.all_to_all(packed, plane, 0, 0)  31.3 us
    all_to_all x1, blocking collectives, shards(): summed = lax.all_to_all(slices, 'row', 0, 0).sum(0)  21.8 us
    pallas_call x1, Pallas kernels, inverse_factor(): pl.pallas_call(factor_kernel, out_shape=jax.ShapeDtypeStruct((NP, NP), F3...  21.3 us
    all_to_all x1, blocking collectives, shards(): near = lax.all_to_all(copies(summed, places), plane, 0, 0)  15.2 us
    pallas_call x1, Pallas kernels, project(): pl.pallas_call(project_kernel, grid_spec=pltpu.PrefetchScalarGridSpec(num...  15 us
    pallas_call x2, Pallas kernels, moments(): pl.pallas_call(functools.partial(moments_kernel, second, sub), grid_spec=...  14.9 us
    psum x1, waiting for transfers between devices, shards(): cross = lax.psum(cross, 'row')  10.4 us
    pallas_call x1, Pallas kernels, basis_of(): pl.pallas_call(basis_kernel, grid=(halves, epochs // rows), in_specs=[pl....  6.97 us
  transfers between devices with their start and end apart: 2, of which 1 were waited for; matrix products, arithmetic and copies ran while one was open for 0% of the time, Pallas kernels for 22%

profile of v1, /device:TPU:2, one launch (start us, length us, event | category | flops | bytes accessed | tf_op | source)
XLA Modules:
  0.0 160.3 jit_solution(4453609613999857809)
XLA Ops:
  7.2 0.0 all-reduce.2.cloned.1.call-start
  7.2 0.7 slice_bitcast_fusion.1
  7.9 1.8 %all-gather.1 = s32[2,2,512]{2,1,0:T(2,128)S(1)} all-gather(s32[1,2,512]{2,1,0:T(2,128)S(1)} %slice_bitcast_fusion.1), channel_id=2, replica_groups=mesh['row'=8,'x'=4,'y'=4,'core'=2] {'core'}, dimensions={0}, use_global_device_ids=true | all-gather | bytes 12288 | tf_op jit(solution)/shard_map/all_gather | solution.py:381
  9.7 0.0 copy-start.1
  9.7 0.7 copy-done.1
  10.3 1.1 pack.1
  11.5 0.0 copy-start
  11.5 31.3 %all_to_all.20.refs_0_.refs_1_ = bf16[16,64,896]{2,1,0:T(8,128)(2,1)S(1)} all-to-all(bf16[16,64,896]{2,1,0:T(8,128)(2,1)S(1)} %pack.1), channel_id=1, replica_groups=mesh['row'=8,'x'=4,'y'=4,'core'=2] {'x','y'}, dimensions={0} | all-to-all | bytes 3670016 | tf_op jit(solution)/shard_map/all_to_all | solution.py:384
  42.8 0.0 collective-permute-start
  42.8 0.0 copy-done
  42.8 0.2 onehots.1
  43.0 6.4 %moments_first.1 = (f32[512,768]{1,0:T(8,128)S(1)}, f32[16,512]{1,0:T(8,128)S(1)}, f32[2,1024,768]{2,1,0:T(8,128)}, bf16[2,1024,512]{2,1,0:T(8,128)(2,1)}, bf16[...) custom-call(s32[1]{0:T(128)} %bitcast.1.mine_ref, ...), custom_call_target="tpu_custom_call" | custom-call | flops 4429185024 | bytes 7077888 | tf_op jit(solution)/shard_map/moments_first/pallas_call | solution.py:188
  49.4 0.0 collective-permute-done.refs_0_
  49.4 8.5 %moments_second.1 = (f32[512,768]{1,0:T(8,128)}, f32[8,16,512]{2,1,0:T(8,128)S(1)}, f32[2,1024,768]{2,1,0:T(8,128)}, bf16[2,1024,512]{2,1,0:T(8,128)(2,1)}, bf16[2,1024,512]{2,1,0:T(8,128)(2,1)}) custom-call(s32[1]{0:T(128)} %bitcast.1.mine_ref, ...), custom_call_target="tpu_custom_call", output_to_operand_aliasing={{2}: (8, {}), {3}: (9, {}), {4}: (10, {})} | custom-call | flops 4429185024 | bytes 7077888 | tf_op jit(solution)/shard_map/moments_second/pallas_call | solution.py:188
  57.9 0.0 all-reduce.2.cloned.1.call-update
  57.9 21.8 %all_to_all.21 = f32[8,16,512]{2,1,0:T(8,128)S(1)} all-to-all(f32[8,16,512]{2,1,0:T(8,128)S(1)} %get-tuple-element.29), channel_id=1, replica_groups=mesh['row'=8,'x'=4,'y'=4,'core'=2] {'row'}, dimensions={0} | all-to-all | bytes 524288 | tf_op jit(solution)/shard_map/all_to_all | solution.py:390
  79.8 0.1 broadcast_in_dim.4
  79.8 15.2 %all_to_all.22 = f32[16,16,512]{2,1,0:T(8,128)S(1)} all-to-all(f32[16,16,512]{2,1,0:T(8,128)S(1)} %broadcast_in_dim.4), channel_id=1, replica_groups=mesh['row'=8,'x'=4,'y'=4,'core'=2] {'x','y'}, dimensions={0} | all-to-all | bytes 1048576 | tf_op jit(solution)/shard_map/all_to_all | solution.py:391
  95.0 0.1 broadcast_in_dim.5
  95.2 4.6 %all_to_all.23.gram_ref = f32[2,16,16,512]{3,2,1,0:T(8,128)S(1)} all-to-all(f32[2,16,16,512]{3,2,1,0:T(8,128)S(1)} %broadcast_in_dim.5), channel_id=1, replica_groups=mesh['row'=8,'x'=4,'y'=4,'core'=2] {'core'}, dimensions={0} | all-to-all | bytes 2097152 | tf_op jit(solution)/shard_map/all_to_all | solution.py:392
  99.7 21.3 %inverse_factor.1.inv_ref = f32[512,512]{1,0:T(8,128)S(1)} custom-call(f32[2,16,16,512]{3,2,1,0:T(8,128)S(1)} %all_to_all.23.gram_ref), custom_call_target="tpu_custom_call" | custom-call | flops 300000000 | bytes 2097152 | tf_op jit(solution)/shard_map/inverse_factor/pallas_call | solution.py:290
  121.1 7.0 %basis_of.1 = (bf16[2,1024,512]{2,1,0:T(8,128)(2,1)}, bf16[2,1024,512]{2,1,0:T(8,128)(2,1)}) custom-call(f32[512,512]{1,0:T(8,128)S(1)} %inverse_factor.1.inv_ref, bf16[2,1024,512]{2,1,0:T(8,128)(2,1)} %get-tuple-element.31.high_ref, bf16[2,1024,512]{2,1,0:T(8,128)(2,1)} %get-tuple-element.32.low_ref), custom_call_target="tpu_custom_call" | custom-call | flops 3221225472 | bytes 8388608 | tf_op jit(solution)/shard_map/basis_of/pallas_call | solution.py:311
  128.1 10.4 %all-reduce.2.cloned.1.call-done.cross_ref = f32[512,768]{1,0:T(8,128)} async-done(((f32[512,768]{1,0:T(8,128)}), f32[512,768]{1,0:T(8,128)}) %all-reduce.2.cloned.1.call-update) | async-done | bytes 1572880 | tf_op jit(solution)/shard_map/psum | solution.py:389
  138.5 15.0 %project.1 = (f32[512,768]{1,0:T(8,128)}, f32[16,2,64,768]{3,2,1,0:T(8,128)}) custom-call(s32[1]{0:T(128)} %bitcast.core_ref, f32[512,512]{1,0:T(8,128)S(1)} %inverse_factor.1.inv_ref, f32[512,768]{1,0:T(8,128)} %all-reduce.2.cloned.1.call-done.cross_ref, bf16[2,1024,512]{2,1,0:T(8,128)(2,1)} %get-tuple-element.33.high_ref, ...), custom_call_target="tpu_custom_call" | custom-call | flops 4831838208 | bytes 16777216 | tf_op jit(solution)/shard_map/project/pallas_call | solution.py:342
  (2 shorter events, 0.0 us)
Async XLA Ops:
  7.2 131.3 %all-reduce.2.cloned.1.call-start = ((), (), s32[]{:S(2)}) async-start(), calls=%async_computation.4 | async-start | bytes 3145728 | tf_op jit(solution)/shard_map/psum | solution.py:389
  9.7 0.7 copy-start.1
  11.5 31.3 %copy-start = (s32[2,768]{1,0:T(2,128)S(1)}, s32[2,768]{1,0:T(2,128)}, u32[]{:S(2)}) copy-start(s32[2,768]{1,0:T(2,128)} %index_ref.1) | copy-start | bytes 18436
  42.8 6.6 %collective-permute-start = (bf16[16,64,896]{2,1,0:T(8,128)(2,1)S(1)}, bf16[16,64,896]{2,1,0:T(8,128)(2,1)}, u32[]{:S(2)}, u32[]{:S(2)}) collective-permute-start(bf16[16,64,896]{2,1,0:T(8,128)(2,1)S(1)} %all_to_all.20.refs_0_.refs_1_), channel_id=1, source_target_pairs={{0,1},{1,0},{2,3},{3,2},{4,5},{5,4},{6,7},{7,6},{8,9},{9,8},{10,11... | collective-permute-start | bytes 5505032 | tf_op jit(solution)/shard_map/ppermute | solution.py:385
Sparse Core Ops, SparseCore 0:
  58.0 80.4 all-reduce.1

commit v2 on v1

--- a/solution.py
+++ b/solution.py
@@ -37,8 +37,7 @@
 def pack_kernel(lat_ref, lon_ref, weight_ref, lead_ref, out_ref, flip):
     flip[...] = jnp.zeros_like(flip)
     flip[0:1, 0:64] = weight_ref[...].astype(F32)
-    lead = lead_ref[...]
-    degree, order = lead[0:1, :], lead[1:2, :]
+    degree, order = lead_ref[0, 0:1, 0:NP], lead_ref[0, 1:2, 0:NP]
     half = order >> 1
     for base, row in ((1, degree), (9, half), (17, order - 2 * half)):
         row = row.astype(F32)
@@ -60,7 +59,7 @@
         scratch_shapes=[pltpu.VMEM((128, 128), F32)],
         compiler_params=pltpu.CompilerParams(vmem_limit_bytes=SMALL_VMEM),
         name="pack",
-    )(*in_hbm(latitude, longitude), weight.reshape(1, -1), lead)
+    )(*in_hbm(latitude, longitude, weight.reshape(1, -1)), lead)
 
 
 def onehot_kernel(index_ref, deg_ref, order_ref):
@@ -80,22 +79,20 @@
     )(index)
 
 
-def moments_kernel(second, sub, mine_ref, *refs):
+def moments_kernel(second, sub, *refs):
     if second:
-        table_ref, deg, order, pdeg, pord, cross_in, slice_in = refs[:7]
-        cross_ref, slices_ref, design_ref, high_ref, low_ref, total = refs[10:]
+        table_ref, deg, order, pdeg, pord, cross_in = refs[:6]
+        cross_ref, design_ref, high_ref, low_ref = refs[9:]
     else:
         head_ref, table_ref, deg, order = refs[:4]
-        cross_ref, total, design_ref, high_ref, low_ref, pdeg, pord = refs[4:]
+        cross_ref, design_ref, high_ref, low_ref, pdeg, pord = refs[4:]
 
     @pl.when(pl.program_id(0) == 0)
     def _():
         if second:
             cross_ref[...] = cross_in[...]
-            total[...] = slice_in[...]
             return
         cross_ref[...] = jnp.zeros_like(cross_ref)
-        total[...] = jnp.zeros_like(total)
         head = head_ref[0].astype(F32)
         lanes = lax.broadcasted_iota(jnp.int32, (64, NDEG), 1).astype(F32)
         wide = lax.broadcasted_iota(jnp.int32, (64, NORD), 1).astype(F32)
@@ -105,8 +102,6 @@
             pdeg[64 * k : 64 * (k + 1), :] = (d == lanes).astype(BF16)
             pord[64 * k : 64 * (k + 1), :] = (o == wide).astype(BF16)
 
-    part = total.shape[0]
-    at = pl.ds(pl.multiple_of(mine_ref[0] * part, part), part)
     last = ((1,), (1,))
 
     def synthesize(k):
@@ -119,17 +114,14 @@
         lat, lon = columns(0, NDEG), columns(NDEG, TAB)
         weight = columns(TAB, WIDE).astype(F32)[:, 0:1]
         high, low = split(weight * dot(lat, pdeg[...], last) * dot(lon, pord[...], last))
-        own = split(weight * dot(lat, pdeg[at, :], last) * dot(lon, pord[at, :], last))
         high_ref[0, rows, :], low_ref[0, rows, :] = high, low
         design = weight * dot(lat, deg[...]) * dot(lon, order[...])
         design_ref[0, rows, :] = design
-        return high, low, own, split(design)
-
-    def accumulate(high, low, own, design):
+        return high, low, split(design)
+
+    def accumulate(high, low, design):
         lhs = jnp.concatenate([high.T, high.T, low.T], axis=1)
         cross_ref[...] += dot(lhs, jnp.concatenate([design[0], design[1], design[0]], axis=0))
-        lhs = jnp.concatenate([own[0].T, own[0].T, own[1].T], axis=1)
-        total[...] += dot(lhs, jnp.concatenate([high, low, high], axis=0))
 
     count = high_ref.shape[1] // sub
     ready = synthesize(0)
@@ -137,59 +129,47 @@
         following = synthesize(k + 1) if k + 1 < count else None
         accumulate(*ready)
         ready = following
-    if second:
-        for k in range(slices_ref.shape[0]):
-            slices_ref[k] = total[...]
-
-
-def moments(table, deg, order, mine, part, rows_of, prior=None, rows=512, sub=256):
+
+
+def moments(table, deg, order, prior=None, rows=512, sub=256):
     epochs, cols = 64 * table.shape[0], deg.shape[1]
-    steps = epochs // rows
     second = prior is not None
     half = 1 if second else 0
-    whole = lambda i, s: (0, 0)
-    along = lambda i, s: (half, i, 0)
-    table_spec = pl.BlockSpec((rows // 64, 64, WIDE), lambda i, s: (i, 0, 0))
+    whole = lambda i: (0, 0)
+    along = lambda i: (half, i, 0)
+    table_spec = pl.BlockSpec((rows // 64, 64, WIDE), lambda i: (i, 0, 0))
     fixed = [pl.BlockSpec(x.shape, whole) for x in (deg, order)]
-    pdeg_spec, pord_spec = pl.BlockSpec((NP, NDEG), whole), pl.BlockSpec((NP, NORD), whole)
-    cross_spec, slice_spec = pl.BlockSpec((NP, cols), whole), pl.BlockSpec((part, NP), whole)
-    big_specs = [
-        pl.BlockSpec((1, rows, cols), along),
-        pl.BlockSpec((1, rows, NP), along),
-        pl.BlockSpec((1, rows, NP), along),
-    ]
+    panel_specs = [pl.BlockSpec((NP, NDEG), whole), pl.BlockSpec((NP, NORD), whole)]
+    cross_spec = pl.BlockSpec((NP, cols), whole)
+    big_specs = [pl.BlockSpec((1, rows, width), along) for width in (cols, NP, NP)]
     big_shapes = [
         pltpu.HBM((2, epochs, cols), F32),
         pltpu.HBM((2, epochs, NP), BF16),
         pltpu.HBM((2, epochs, NP), BF16),
     ]
-    cross_shape = (pltpu.HBM if second else jax.ShapeDtypeStruct)((NP, cols), F32)
     if second:
-        cross, total, design, high, low, pdeg, pord = prior
-        args = (table, deg, order, pdeg, pord, cross, total, *in_hbm(design, high, low))
-        in_specs = [table_spec, *fixed, pdeg_spec, pord_spec, cross_spec, slice_spec]
-        in_specs += [pl.BlockSpec(memory_space=pl.ANY)] * 3
-        out_specs = [cross_spec, pl.BlockSpec((rows_of, part, NP), lambda i, s: (0, 0, 0)), *big_specs]
-        out_shape = [cross_shape, jax.ShapeDtypeStruct((rows_of, part, NP), F32), *big_shapes]
-        scratch = [pltpu.VMEM((part, NP), F32)]
-        aliases = {8: 2, 9: 3, 10: 4}
+        cross, design, high, low, pdeg, pord = prior
+        args = (table, deg, order, pdeg, pord, cross, *in_hbm(design, high, low))
+        in_specs = [table_spec, *fixed, *panel_specs, cross_spec] + [pl.BlockSpec(memory_space=pl.ANY)] * 3
+        out_specs = [cross_spec, *big_specs]
+        out_shape = [pltpu.HBM((NP, cols), F32), *big_shapes]
+        aliases = {6: 1, 7: 2, 8: 3}
     else:
         args = (table, table, deg, order)
-        in_specs = [pl.BlockSpec((1, 64, 128), lambda i, s: (0, 0, TAB // 128)), table_spec, *fixed]
-        out_specs = [cross_spec, slice_spec, *big_specs, pdeg_spec, pord_spec]
+        in_specs = [pl.BlockSpec((1, 64, 128), lambda i: (0, 0, TAB // 128)), table_spec, *fixed]
+        out_specs = [cross_spec, *big_specs, *panel_specs]
         out_shape = [
-            cross_shape,
-            jax.ShapeDtypeStruct((part, NP), F32),
+            jax.ShapeDtypeStruct((NP, cols), F32),
             *big_shapes,
             jax.ShapeDtypeStruct((NP, NDEG), BF16),
             jax.ShapeDtypeStruct((NP, NORD), BF16),
         ]
-        scratch, aliases = [], {}
+        aliases = {}
     return pl.pallas_call(
         functools.partial(moments_kernel, second, sub),
-        grid_spec=pltpu.PrefetchScalarGridSpec(
-            num_scalar_prefetch=1, grid=(steps,), in_specs=in_specs, out_specs=out_specs, scratch_shapes=scratch
-        ),
+        grid=(epochs // rows,),
+        in_specs=in_specs,
+        out_specs=out_specs,
         out_shape=out_shape,
         input_output_aliases=aliases,
         compiler_params=pltpu.CompilerParams(vmem_limit_bytes=VMEM_LIMIT),
@@ -199,7 +179,50 @@
             transcendentals=0,
         ),
         name="moments_second" if second else "moments_first",
-    )(mine, *args)
+    )(*args)
+
+
+def slices_kernel(mine_ref, high_ref, low_ref, out_ref, total):
+    first = (pl.program_id(0) == 0) & (pl.program_id(1) == 0)
+    part = total.shape[0]
+    row = mine_ref[0] * part + lax.broadcasted_iota(jnp.int32, (NP, part), 1)
+    pick = (lax.broadcasted_iota(jnp.int32, (NP, part), 0) == row).astype(BF16)
+    high, low = high_ref[0], low_ref[0]
+    own_high, own_low = dot(high, pick).astype(BF16), dot(low, pick).astype(BF16)
+    lhs = jnp.concatenate([own_high.T, own_high.T, own_low.T], axis=1)
+    added = dot(lhs, jnp.concatenate([high, low, high], axis=0))
+
+    @pl.when(first)
+    def _():
+        total[...] = added
+
+    @pl.when(jnp.logical_not(first))
+    def _():
+        total[...] += added
+
+    for k in range(out_ref.shape[0]):
+        out_ref[k] = total[...]
+
+
+def gram_slices(mine, high, low, part, count, rows=1024):
+    halves, epochs = high.shape[:2]
+    spec = pl.BlockSpec((1, rows, NP), lambda h, i, s: (h, i, 0))
+    return pl.pallas_call(
+        slices_kernel,
+        grid_spec=pltpu.PrefetchScalarGridSpec(
+            num_scalar_prefetch=1,
+            grid=(halves, epochs // rows),
+            in_specs=[spec, spec],
+            out_specs=pl.BlockSpec((count, part, NP), lambda h, i, s: (0, 0, 0)),
+            scratch_shapes=[pltpu.VMEM((part, NP), F32)],
+        ),
+        out_shape=jax.ShapeDtypeStruct((count, part, NP), F32),
+        compiler_params=pltpu.CompilerParams(vmem_limit_bytes=SMALL_VMEM),
+        cost_estimate=pl.CostEstimate(
+            flops=12 * epochs * part * NP, bytes_accessed=8 * epochs * NP, transcendentals=0
+        ),
+        name="gram_slices",
+    )(mine, *in_hbm(high, low))
 
 
 def invert_block(s_ref, t_ref, x_ref):
@@ -297,23 +320,27 @@
     )(gram)
 
 
-def basis_kernel(inv_ref, high_ref, low_ref, qhigh_ref, qlow_ref):
-    xhigh, xlow = split(inv_ref[...])
+def basis_kernel(inv_ref, high_ref, low_ref, qhigh_ref, qlow_ref, xhigh_ref, xlow_ref):
+    @pl.when((pl.program_id(0) == 0) & (pl.program_id(1) == 0))
+    def _():
+        xhigh_ref[...], xlow_ref[...] = split(inv_ref[...])
+
     last = ((1,), (1,))
-    high = high_ref[0]
-    basis = dot(high, xhigh, last) + dot(high, xlow, last) + dot(low_ref[0], xhigh, last)
+    high, xhigh = high_ref[0], xhigh_ref[...]
+    basis = dot(high, xhigh, last) + dot(high, xlow_ref[...], last) + dot(low_ref[0], xhigh, last)
     qhigh_ref[0], qlow_ref[0] = split(basis)
 
 
 def basis_of(inv, high, low, rows=512):
     halves, epochs = high.shape[:2]
     spec = pl.BlockSpec((1, rows, NP), lambda h, i: (h, i, 0))
+    whole = pl.BlockSpec((NP, NP), lambda h, i: (0, 0))
     return pl.pallas_call(
         basis_kernel,
         grid=(halves, epochs // rows),
-        in_specs=[pl.BlockSpec((NP, NP), lambda h, i: (0, 0)), spec, spec],
-        out_specs=[spec, spec],
-        out_shape=[pltpu.HBM(high.shape, BF16)] * 2,
+        in_specs=[whole, spec, spec],
+        out_specs=[spec, spec, whole, whole],
+        out_shape=[pltpu.VMEM(high.shape, BF16), pltpu.HBM(high.shape, BF16)] + [pltpu.VMEM((NP, NP), BF16)] * 2,
         compiler_params=pltpu.CompilerParams(vmem_limit_bytes=SMALL_VMEM),
         cost_estimate=pl.CostEstimate(
             flops=12 * epochs * NP * NP, bytes_accessed=16 * epochs * NP, transcendentals=0
@@ -322,51 +349,56 @@
     )(inv, *in_hbm(high, low))
 
 
-def project_kernel(core_ref, inv_ref, cross_ref, high_ref, low_ref, design_ref, coef_ref, rest_ref, chigh, clow):
-    @pl.when((pl.program_id(0) == 0) & (pl.program_id(1) == 0))
+def project_kernel(core_ref, xhigh, xlow, qhigh, cross_ref, qlow_ref, design_ref, coef_ref, rest_ref, both):
+    h, i = pl.program_id(0), pl.program_id(1)
+
+    @pl.when((h == 0) & (i == 0))
     def _():
-        coef = dot(inv_ref[...], cross_ref[...], precision=HIGHEST)
+        high, low = split(cross_ref[...])
+        coef = dot(xhigh[...], high) + dot(xhigh[...], low) + dot(xlow[...], high)
         coef_ref[...] = coef
-        chigh[...], clow[...] = split(coef)
-
-    high = high_ref[0]
-    rest = design_ref[0] - (dot(high, chigh[...]) + dot(high, clow[...]) + dot(low_ref[0], chigh[...]))
-    rest_ref[...] = rest.reshape(rest_ref.shape)
-
-
-def project(core, inv, cross, high, low, design, rows=256):
+        both[0:NP, :], both[NP : 2 * NP, :] = split(coef)
+
+    rows = design_ref.shape[1]
+    high = qhigh[h, pl.ds(pl.multiple_of(i * rows, rows), rows), :]
+    span = dot(jnp.concatenate([high, high], axis=1), both[...]) + dot(qlow_ref[0], both[0:NP, :])
+    rest_ref[...] = (design_ref[0] - span).reshape(rest_ref.shape)
+
+
+def project(core, xhigh, xlow, cross, high, low, design, rows=512):
     halves, epochs, cols = design.shape
-    whole = lambda h, i, s: (0, 0)
+    here = pl.BlockSpec(memory_space=pltpu.VMEM)
+    whole = pl.BlockSpec((NP, cols), lambda h, i, s: (0, 0))
     along = lambda h, i, s: (h, i, 0)
-    tall = rows // 64
     return pl.pallas_call(
         project_kernel,
         grid_spec=pltpu.PrefetchScalarGridSpec(
             num_scalar_prefetch=1,
             grid=(halves, epochs // rows),
             in_specs=[
-                pl.BlockSpec((NP, NP), whole),
-                pl.BlockSpec((NP, cols), whole),
-                pl.BlockSpec((1, rows, NP), along),
+                here,
+                here,
+                here,
+                whole,
                 pl.BlockSpec((1, rows, NP), along),
                 pl.BlockSpec((1, rows, cols), along),
             ],
             out_specs=[
-                pl.BlockSpec((NP, cols), whole),
-                pl.BlockSpec((tall, 1, 64, cols), lambda h, i, s: (i, (s[0] + h) % 2, 0, 0)),
+                whole,
+                pl.BlockSpec((rows // 64, 1, 64, cols), lambda h, i, s: (i, (s[0] + h) % 2, 0, 0)),
             ],
-            scratch_shapes=[pltpu.VMEM((NP, cols), BF16), pltpu.VMEM((NP, cols), BF16)],
+            scratch_shapes=[pltpu.VMEM((2 * NP, cols), BF16)],
         ),
         out_shape=[
             jax.ShapeDtypeStruct((NP, cols), F32),
             jax.ShapeDtypeStruct((epochs // 64, halves, 64, cols), F32),
         ],
-        compiler_params=pltpu.CompilerParams(vmem_limit_bytes=SMALL_VMEM),
+        compiler_params=pltpu.CompilerParams(vmem_limit_bytes=VMEM_LIMIT),
         cost_estimate=pl.CostEstimate(
             flops=12 * epochs * cols * NP, bytes_accessed=2 * epochs * (8 * cols + 4 * NP), transcendentals=0
         ),
         name="project",
-    )(core, inv, *in_hbm(cross, high, low, design))
+    )(core, xhigh, xlow, high, *in_hbm(cross, low, design))
 
 
 def copies(x, count):
@@ -378,21 +410,21 @@
     places = lax.axis_size("x") * lax.axis_size("y")
     core = lax.axis_index("core")
     mine = (lax.axis_index(plane) * cores + core).reshape(1)
-    lead = lax.all_gather(harmonic_index[:, :NP], "core")[0]
+    lead = lax.all_gather(harmonic_index, "core")
     packed = pack(latitude, longitude, weight, lead, places)
     deg, order = onehots(harmonic_index)
     own = lax.all_to_all(packed, plane, 0, 0)
     other = lax.ppermute(own, "core", [(k, (k + 1) % cores) for k in range(cores)])
     part = NP // (places * cores)
-    first = moments(own, deg, order, mine, part, nrow)
-    cross, slices, design, high, low = moments(other, deg, order, mine, part, nrow, first)
+    cross, design, high, low = moments(other, deg, order, moments(own, deg, order))
     cross = lax.psum(cross, "row")
+    slices = gram_slices(mine, high, low, part, nrow)
     summed = lax.all_to_all(slices, "row", 0, 0).sum(0)
     near = lax.all_to_all(copies(summed, places), plane, 0, 0)
     gram = lax.all_to_all(copies(near, cores), "core", 0, 0)
     inv = inverse_factor(gram)
-    qhigh, qlow = basis_of(inv, high, low)
-    coefficients, rest = project(core.reshape(1), inv, cross, qhigh, qlow, design)
+    qhigh, qlow, xhigh, xlow = basis_of(inv, high, low)
+    coefficients, rest = project(core.reshape(1), xhigh, xlow, cross, qhigh, qlow, design)
     return coefficients, rest.reshape(-1, rest.shape[-1])
 
 

time: 161 us -> 157 us (0.975)
  Pallas kernels: 59.5 us -> 56.1 us
    pallas_call x1, Pallas kernels: 15 us -> 11.2 us  [project(): pl.pallas_call(project_kernel, grid_spec=pltpu.PrefetchScalarGridSpec(num...]
    all_to_all x1, blocking collectives: 21.8 us -> 23.8 us  [shards(): summed = lax.all_to_all(slices, 'row', 0, 0).sum(0)]
    pallas_call x3 -> x4, Pallas kernels: 21.8 us -> 22.3 us  [the longest x2 11.7 us: moments(): pl.pallas_call(functools.partial(moments_kernel, second, sub), grid=(epoc...]
  transfers between devices with their start and end apart: 2 -> 2, of which waited for: 1 -> 1; matrix products, arithmetic and copies ran while one was open for 0% -> 0% of each run, Pallas kernels for 22% -> 24%
where the time goes in v2:
time: 157 us; the launch traced here: 156 us
  blocking collectives  75.6 us (48%)
  Pallas kernels  56.1 us (36%)
  between operations  14.1 us (9%)
  waiting for transfers between devices  9.84 us (6%)
    all_to_all x1, blocking collectives, shards(): own = lax.all_to_all(packed, plane, 0, 0)  31.3 us
    all_to_all x1, blocking collectives, shards(): summed = lax.all_to_all(slices, 'row', 0, 0).sum(0)  23.8 us
    pallas_call x1, Pallas kernels, inverse_factor(): pl.pallas_call(factor_kernel, out_shape=jax.ShapeDtypeStruct((NP, NP), F3...  21.3 us
    all_to_all x1, blocking collectives, shards(): near = lax.all_to_all(copies(summed, places), plane, 0, 0)  14 us
    pallas_call x2, Pallas kernels, moments(): pl.pallas_call(functools.partial(moments_kernel, second, sub), grid=(epoc...  11.7 us
    pallas_call x1, Pallas kernels, project(): pl.pallas_call(project_kernel, grid_spec=pltpu.PrefetchScalarGridSpec(num...  11.2 us
    psum x1, waiting for transfers between devices, shards(): cross = lax.psum(cross, 'row')  9.83 us
    pallas_call x1, Pallas kernels, basis_of(): pl.pallas_call(basis_kernel, grid=(halves, epochs // rows), in_specs=[who...  6.75 us
  transfers between devices with their start and end apart: 2, of which 1 were waited for; matrix products, arithmetic and copies ran while one was open for 0% of the time, Pallas kernels for 24%

profile of v2, /device:TPU:2, one launch (start us, length us, event | category | flops | bytes accessed | tf_op | source)
XLA Modules:
  0.0 156.0 jit_solution(2575838726857236285)
XLA Ops:
  7.2 0.0 all-reduce.2.cloned.1.call-start
  7.2 2.0 %all-gather.1.lead_ref = s32[2,2,768]{2,1,0:T(2,128)S(1)} all-gather(s32[1,2,768]{2,1,0:T(2,128)} %bitcast.5), channel_id=2, replica_groups=mesh['row'=8,'x'=4,'y'=4,'core'=2] {'core'}, dimensions={0}, use_global_device_ids=true | all-gather | bytes 18432 | tf_op jit(solution)/shard_map/all_gather | solution.py:413
  9.2 1.1 pack.1
  10.4 0.0 copy-start
  10.4 31.3 %all_to_all.20.refs_0_.refs_1_ = bf16[16,64,896]{2,1,0:T(8,128)(2,1)S(1)} all-to-all(bf16[16,64,896]{2,1,0:T(8,128)(2,1)S(1)} %pack.1), channel_id=1, replica_groups=mesh['row'=8,'x'=4,'y'=4,'core'=2] {'x','y'}, dimensions={0} | all-to-all | bytes 3670016 | tf_op jit(solution)/shard_map/all_to_all | solution.py:416
  41.6 0.0 collective-permute-start
  41.6 0.0 copy-done
  41.6 0.2 onehots.1
  41.8 5.4 %moments_first.1 = (f32[512,768]{1,0:T(8,128)S(1)}, f32[2,1024,768]{2,1,0:T(8,128)}, bf16[2,1024,512]{2,1,0:T(8,128)(2,1)}, bf16[2,1024,512]{2,1,0:T(8,128)(2,1)...) custom-call(bf16[16,64,896]{2,1,0:T(8,128)(2,1)S(1)} %all_to_all.20.refs_0_.refs_1_, ...), custom_call_target="tpu_custom_call" | custom-call | flops 4429185024 | bytes 7077888 | tf_op jit(solution)/shard_map/moments_first/pallas_call | solution.py:168
  47.3 0.0 collective-permute-done.refs_0_
  47.3 6.2 %moments_second.1 = (f32[512,768]{1,0:T(8,128)}, f32[2,1024,768]{2,1,0:T(8,128)}, bf16[2,1024,512]{2,1,0:T(8,128)(2,1)}, bf16[2,1024,512]{2,1,0:T(8,128)(2,1)}) custom-call(bf16[16,64,896]{2,1,0:T(8,128)(2,1)S(1)} %collective-permute-done.refs_0_, ...), custom_call_target="tpu_custom_call", output_to_operand_aliasing={{1}: (6, {}), {2}: (7, {}), {3}: (8, {})} | custom-call | flops 4429185024 | bytes 7077888 | tf_op jit(solution)/shard_map/moments_second/pallas_call | solution.py:168
  53.5 0.0 all-reduce.2.cloned.1.call-update
  53.5 3.9 %gram_slices.1 = f32[8,16,512]{2,1,0:T(8,128)S(1)} custom-call(s32[1]{0:T(128)} %bitcast.1.mine_ref, bf16[2,1024,512]{2,1,0:T(8,128)(2,1)} %get-tuple-element.28.high_ref, bf16[2,1024,512]{2,1,0:T(8,128)(2,1)} %get-tuple-element.29.low_ref), custom_call_target="tpu_custom_call" | custom-call | flops 100663296 | bytes 4194304 | tf_op jit(solution)/shard_map/gram_slices/pallas_call | solution.py:210
  57.5 23.8 %all_to_all.21 = f32[8,16,512]{2,1,0:T(8,128)S(1)} all-to-all(f32[8,16,512]{2,1,0:T(8,128)S(1)} %gram_slices.1), channel_id=1, replica_groups=mesh['row'=8,'x'=4,'y'=4,'core'=2] {'row'}, dimensions={0} | all-to-all | bytes 524288 | tf_op jit(solution)/shard_map/all_to_all | solution.py:422
  81.3 0.1 broadcast_in_dim.4
  81.3 14.0 %all_to_all.22 = f32[16,16,512]{2,1,0:T(8,128)S(1)} all-to-all(f32[16,16,512]{2,1,0:T(8,128)S(1)} %broadcast_in_dim.4), channel_id=1, replica_groups=mesh['row'=8,'x'=4,'y'=4,'core'=2] {'x','y'}, dimensions={0} | all-to-all | bytes 1048576 | tf_op jit(solution)/shard_map/all_to_all | solution.py:423
  95.3 0.1 broadcast_in_dim.5
  95.4 4.6 %all_to_all.23.gram_ref = f32[2,16,16,512]{3,2,1,0:T(8,128)S(1)} all-to-all(f32[2,16,16,512]{3,2,1,0:T(8,128)S(1)} %broadcast_in_dim.5), channel_id=1, replica_groups=mesh['row'=8,'x'=4,'y'=4,'core'=2] {'core'}, dimensions={0} | all-to-all | bytes 2097152 | tf_op jit(solution)/shard_map/all_to_all | solution.py:424
  100.0 21.3 %inverse_factor.1.inv_ref = f32[512,512]{1,0:T(8,128)S(1)} custom-call(f32[2,16,16,512]{3,2,1,0:T(8,128)S(1)} %all_to_all.23.gram_ref), custom_call_target="tpu_custom_call" | custom-call | flops 300000000 | bytes 2097152 | tf_op jit(solution)/shard_map/inverse_factor/pallas_call | solution.py:313
  121.4 6.8 %basis_of.1 = (bf16[2,1024,512]{2,1,0:T(8,128)(2,1)S(1)}, bf16[2,1024,512]{2,1,0:T(8,128)(2,1)}, bf16[512,512]{1,0:T(8,128)(2,1)S(1)}, bf16[512,512]{1,0:T(8,128)(2,1)S(1)}) custom-call(f32[512,512]{1,0:T(8,128)S(1)} %inverse_factor.1.inv_ref, bf16[2,1024,512]{2,1,0:T(8,128)(2,1)} %get-tuple-element.28.high_ref, bf16[2,1024,512]{2,1,0:T(8,128)(2,1)} %get-tuple-element.29.low_ref), custom_call_target="tpu_custom_call" | custom-call | flops 3221225472 | bytes 8388608 | tf_op jit(solution)/shard_map/basis_of/pallas_call | solution.py:338
  128.1 9.8 %all-reduce.2.cloned.1.call-done.cross_ref = f32[512,768]{1,0:T(8,128)} async-done(((f32[512,768]{1,0:T(8,128)}), f32[512,768]{1,0:T(8,128)}) %all-reduce.2.cloned.1.call-update) | async-done | bytes 1572880 | tf_op jit(solution)/shard_map/psum | solution.py:420
  137.9 11.2 %project.1 = (f32[512,768]{1,0:T(8,128)}, f32[16,2,64,768]{3,2,1,0:T(8,128)}) custom-call(s32[1]{0:T(128)} %bitcast.core_ref, bf16[512,512]{1,0:T(8,128)(2,1)S(1)} %get-tuple-element.30.xhigh, bf16[512,512]{1,0:T(8,128)(2,1)S(1)} %get-tuple-element.31.xlow, bf16[2,1024,512]{2,1,0:T(8,128)(2,1)S(1)} %get-tuple-element.32.qhigh, ...), custom_call_target="tpu_custom_call" | custom-call | flops 4831838208 | bytes 16777216 | tf_op jit(solution)/shard_map/project/pallas_call | solution.py:373
  (1 shorter events, 0.0 us)
Async XLA Ops:
  7.2 130.8 %all-reduce.2.cloned.1.call-start = ((), (), s32[]{:S(2)}) async-start(), calls=%async_computation.4 | async-start | bytes 3145728 | tf_op jit(solution)/shard_map/psum | solution.py:420
  10.4 31.3 %copy-start = (s32[2,768]{1,0:T(2,128)S(1)}, s32[2,768]{1,0:T(2,128)}, u32[]{:S(2)}) copy-start(s32[2,768]{1,0:T(2,128)} %index_ref.1) | copy-start | bytes 18436
  41.6 5.7 %collective-permute-start = (bf16[16,64,896]{2,1,0:T(8,128)(2,1)S(1)}, bf16[16,64,896]{2,1,0:T(8,128)(2,1)S(1)}, u32[]{:S(2)}, u32[]{:S(2)}) collective-permute-start(bf16[16,64,896]{2,1,0:T(8,128)(2,1)S(1)} %all_to_all.20.refs_0_.refs_1_), channel_id=1, source_target_pairs={{0,1},{1,0},{2,3},{3,2},{4,5},{5,4},{6,7},{7,6},{8,9},{9,8},{10,11... | collective-permute-start | bytes 5505032 | tf_op jit(solution)/shard_map/ppermute | solution.py:417
Sparse Core Ops, SparseCore 0:
  53.7 84.2 all-reduce.1

commit v3 on v2

--- a/solution.py
+++ b/solution.py
@@ -182,7 +182,7 @@
     )(*args)
 
 
-def slices_kernel(mine_ref, high_ref, low_ref, out_ref, total):
+def slice_kernel(mine_ref, high_ref, low_ref, out_ref, total):
     first = (pl.program_id(0) == 0) & (pl.program_id(1) == 0)
     part = total.shape[0]
     row = mine_ref[0] * part + lax.broadcasted_iota(jnp.int32, (NP, part), 1)
@@ -200,28 +200,27 @@
     def _():
         total[...] += added
 
-    for k in range(out_ref.shape[0]):
-        out_ref[k] = total[...]
-
-
-def gram_slices(mine, high, low, part, count, rows=1024):
+    out_ref[...] = total[...]
+
+
+def gram_slice(mine, high, low, part, rows=1024):
     halves, epochs = high.shape[:2]
     spec = pl.BlockSpec((1, rows, NP), lambda h, i, s: (h, i, 0))
     return pl.pallas_call(
-        slices_kernel,
+        slice_kernel,
         grid_spec=pltpu.PrefetchScalarGridSpec(
             num_scalar_prefetch=1,
             grid=(halves, epochs // rows),
             in_specs=[spec, spec],
-            out_specs=pl.BlockSpec((count, part, NP), lambda h, i, s: (0, 0, 0)),
+            out_specs=pl.BlockSpec((part, NP), lambda h, i, s: (0, 0)),
             scratch_shapes=[pltpu.VMEM((part, NP), F32)],
         ),
-        out_shape=jax.ShapeDtypeStruct((count, part, NP), F32),
+        out_shape=jax.ShapeDtypeStruct((part, NP), F32),
         compiler_params=pltpu.CompilerParams(vmem_limit_bytes=SMALL_VMEM),
         cost_estimate=pl.CostEstimate(
             flops=12 * epochs * part * NP, bytes_accessed=8 * epochs * NP, transcendentals=0
         ),
-        name="gram_slices",
+        name="gram_slice",
     )(mine, *in_hbm(high, low))
 
 
@@ -349,20 +348,27 @@
     )(inv, *in_hbm(high, low))
 
 
-def project_kernel(core_ref, xhigh, xlow, qhigh, cross_ref, qlow_ref, design_ref, coef_ref, rest_ref, both):
+def project_kernel(core_ref, xhigh, xlow, qhigh, cross_ref, qlow_ref, design_ref, coef_hbm, rest_ref,
+                   coef_ref, both, sem):
     h, i = pl.program_id(0), pl.program_id(1)
+    put = pltpu.make_async_copy(coef_ref, coef_hbm, sem)
 
     @pl.when((h == 0) & (i == 0))
     def _():
         high, low = split(cross_ref[...])
         coef = dot(xhigh[...], high) + dot(xhigh[...], low) + dot(xlow[...], high)
         coef_ref[...] = coef
+        put.start()
         both[0:NP, :], both[NP : 2 * NP, :] = split(coef)
 
     rows = design_ref.shape[1]
     high = qhigh[h, pl.ds(pl.multiple_of(i * rows, rows), rows), :]
     span = dot(jnp.concatenate([high, high], axis=1), both[...]) + dot(qlow_ref[0], both[0:NP, :])
     rest_ref[...] = (design_ref[0] - span).reshape(rest_ref.shape)
+
+    @pl.when((h == pl.num_programs(0) - 1) & (i == pl.num_programs(1) - 1))
+    def _():
+        put.wait()
 
 
 def project(core, xhigh, xlow, cross, high, low, design, rows=512):
@@ -384,13 +390,17 @@
                 pl.BlockSpec((1, rows, cols), along),
             ],
             out_specs=[
-                whole,
+                pl.BlockSpec(memory_space=pl.ANY),
                 pl.BlockSpec((rows // 64, 1, 64, cols), lambda h, i, s: (i, (s[0] + h) % 2, 0, 0)),
             ],
-            scratch_shapes=[pltpu.VMEM((2 * NP, cols), BF16)],
+            scratch_shapes=[
+                pltpu.VMEM((NP, cols), F32),
+                pltpu.VMEM((2 * NP, cols), BF16),
+                pltpu.SemaphoreType.DMA,
+            ],
         ),
         out_shape=[
-            jax.ShapeDtypeStruct((NP, cols), F32),
+            pltpu.HBM((NP, cols), F32),
             jax.ShapeDtypeStruct((epochs // 64, halves, 64, cols), F32),
         ],
         compiler_params=pltpu.CompilerParams(vmem_limit_bytes=VMEM_LIMIT),
@@ -418,8 +428,11 @@
     part = NP // (places * cores)
     cross, design, high, low = moments(other, deg, order, moments(own, deg, order))
     cross = lax.psum(cross, "row")
-    slices = gram_slices(mine, high, low, part, nrow)
-    summed = lax.all_to_all(slices, "row", 0, 0).sum(0)
+    summed = gram_slice(mine, high, low, part)
+    hop = 1
+    while hop < nrow:
+        summed = summed + lax.ppermute(summed, "row", [(k, k ^ hop) for k in range(nrow)])
+        hop *= 2
     near = lax.all_to_all(copies(summed, places), plane, 0, 0)
     gram = lax.all_to_all(copies(near, cores), "core", 0, 0)
     inv = inverse_factor(gram)

time: 157 us -> 153 us (0.975)
  blocking collectives: 75.6 us -> 50.4 us
  starting transfers between devices: 0.04 us -> 12.4 us
  waiting for transfers between devices: 9.84 us -> 19.4 us
    all_to_all x1 -> x0, blocking collectives: 23.8 us -> none  [shards(): summed = lax.all_to_all(slices, 'row', 0, 0).sum(0)]
    ppermute x0 -> x3, starting transfers between devices: none -> 12.3 us  [shards(): lax.ppermute(summed, 'row', [(k, k ^ hop) for k in range(nrow)])]
    ppermute x0 -> x3, waiting for transfers between devices: none -> 6.65 us  [shards(): lax.ppermute(summed, 'row', [(k, k ^ hop) for k in range(nrow)])]
    psum x1, waiting for transfers between devices: 9.83 us -> 12.7 us  [shards(): cross = lax.psum(cross, 'row')]
  transfers between devices with their start and end apart: 2 -> 5, of which waited for: 1 -> 4; matrix products, arithmetic and copies ran while one was open for 0% -> 0% of each run, Pallas kernels for 24% -> 25%
where the time goes in v3:
time: 153 us
  Pallas kernels  56.1 us (37%)
  blocking collectives  50.4 us (33%)
  waiting for transfers between devices  19.4 us (13%)
  between operations  14.1 us (9%)
  starting transfers between devices  12.4 us (8%)
    all_to_all x1, blocking collectives, shards(): own = lax.all_to_all(packed, plane, 0, 0)  31.3 us
    pallas_call x1, Pallas kernels, inverse_factor(): pl.pallas_call(factor_kernel, out_shape=jax.ShapeDtypeStruct((NP, NP), F3...  21.3 us
    psum x1, waiting for transfers between devices, shards(): cross = lax.psum(cross, 'row')  12.7 us
    all_to_all x1, blocking collectives, shards(): near = lax.all_to_all(copies(summed, places), plane, 0, 0)  12.5 us
    ppermute x3, starting transfers between devices, shards(): lax.ppermute(summed, 'row', [(k, k ^ hop) for k in range(nrow)])  12.3 us
    pallas_call x2, Pallas kernels, moments(): pl.pallas_call(functools.partial(moments_kernel, second, sub), grid=(epoc...  11.7 us
    pallas_call x1, Pallas kernels, project(): pl.pallas_call(project_kernel, grid_spec=pltpu.PrefetchScalarGridSpec(num...  11.2 us
    pallas_call x1, Pallas kernels, basis_of(): pl.pallas_call(basis_kernel, grid=(halves, epochs // rows), in_specs=[who...  6.78 us
  transfers between devices with their start and end apart: 5, of which 4 were waited for; matrix products, arithmetic and copies ran while one was open for 0% of the time, Pallas kernels for 25%

profile of v3, /device:TPU:2, one launch (start us, length us, event | category | flops | bytes accessed | tf_op | source)
XLA Modules:
  0.0 152.5 jit_solution(5210806010261078911)
XLA Ops:
  7.2 0.0 all-reduce.2.cloned.1.call-start
  7.2 2.0 %all-gather.1.lead_ref = s32[2,2,768]{2,1,0:T(2,128)S(1)} all-gather(s32[1,2,768]{2,1,0:T(2,128)} %bitcast.5), channel_id=2, replica_groups=mesh['row'=8,'x'=4,'y'=4,'core'=2] {'core'}, dimensions={0}, use_global_device_ids=true | all-gather | bytes 18432 | tf_op jit(solution)/shard_map/all_gather | solution.py:423
  9.2 1.1 pack.1
  10.4 0.0 copy-start
  10.4 31.3 %all_to_all.15.refs_0_.refs_1_ = bf16[16,64,896]{2,1,0:T(8,128)(2,1)S(1)} all-to-all(bf16[16,64,896]{2,1,0:T(8,128)(2,1)S(1)} %pack.1), channel_id=1, replica_groups=mesh['row'=8,'x'=4,'y'=4,'core'=2] {'x','y'}, dimensions={0} | all-to-all | bytes 3670016 | tf_op jit(solution)/shard_map/all_to_all | solution.py:426
  41.6 0.0 collective-permute-start
  41.6 0.0 copy-done
  41.6 0.2 onehots.1
  41.8 5.4 %moments_first.1 = (f32[512,768]{1,0:T(8,128)S(1)}, f32[2,1024,768]{2,1,0:T(8,128)}, bf16[2,1024,512]{2,1,0:T(8,128)(2,1)}, bf16[2,1024,512]{2,1,0:T(8,128)(2,1)...) custom-call(bf16[16,64,896]{2,1,0:T(8,128)(2,1)S(1)} %all_to_all.15.refs_0_.refs_1_, ...), custom_call_target="tpu_custom_call" | custom-call | flops 4429185024 | bytes 7077888 | tf_op jit(solution)/shard_map/moments_first/pallas_call | solution.py:168
  47.3 0.0 collective-permute-done.refs_0_
  47.3 6.2 %moments_second.1 = (f32[512,768]{1,0:T(8,128)}, f32[2,1024,768]{2,1,0:T(8,128)}, bf16[2,1024,512]{2,1,0:T(8,128)(2,1)}, bf16[2,1024,512]{2,1,0:T(8,128)(2,1)}) custom-call(bf16[16,64,896]{2,1,0:T(8,128)(2,1)S(1)} %collective-permute-done.refs_0_, ...), custom_call_target="tpu_custom_call", output_to_operand_aliasing={{1}: (6, {}), {2}: (7, {}), {3}: (8, {})} | custom-call | flops 4429185024 | bytes 7077888 | tf_op jit(solution)/shard_map/moments_second/pallas_call | solution.py:168
  53.5 0.0 all-reduce.2.cloned.1.call-update
  53.5 3.8 %gram_slice.1 = f32[16,512]{1,0:T(8,128)S(1)} custom-call(s32[1]{0:T(128)} %bitcast.1.mine_ref, bf16[2,1024,512]{2,1,0:T(8,128)(2,1)} %get-tuple-element.28.high_ref, bf16[2,1024,512]{2,1,0:T(8,128)(2,1)} %get-tuple-element.29.low_ref), custom_call_target="tpu_custom_call" | custom-call | flops 100663296 | bytes 4194304 | tf_op jit(solution)/shard_map/gram_slice/pallas_call | solution.py:209
  57.4 2.0 %collective-permute-start.1 = (f32[16,512]{1,0:T(8,128)S(1)}, f32[16,512]{1,0:T(8,128)S(1)}, u32[]{:S(2)}, u32[]{:S(2)}) collective-permute-start(f32[16,512]{1,0:T(8,128)S(1)} %gram_slice.1), channel_id=1, source_target_pairs={{0,32},{32,0},{64,96},{96,64},{128,160},{160,128},{192,224},{224,1... | collective-permute-start | bytes 98312 | tf_op jit(solution)/shard_map/ppermute | solution.py:434
  59.4 2.1 %collective-permute-done.1 = f32[16,512]{1,0:T(8,128)S(1)} collective-permute-done((f32[16,512]{1,0:T(8,128)S(1)}, f32[16,512]{1,0:T(8,128)S(1)}, u32[]{:S(2)}, u32[]{:S(2)}) %collective-permute-start.1) | collective-permute-done | bytes 32800 | tf_op jit(solution)/shard_map/ppermute | solution.py:434
  61.5 3.3 %collective-permute-start.2 = (f32[16,512]{1,0:T(8,128)S(1)}, f32[16,512]{1,0:T(8,128)S(1)}, u32[]{:S(2)}, u32[]{:S(2)}) collective-permute-start(f32[16,512]{1,0:T(8,128)S(1)} %add.19), channel_id=1, source_target_pairs={{0,64},{32,96},{64,0},{96,32},{128,192},{160,224},{192,128},{224,1... | collective-permute-start | bytes 98312 | tf_op jit(solution)/shard_map/ppermute | solution.py:434
  64.7 2.2 %collective-permute-done.2 = f32[16,512]{1,0:T(8,128)S(1)} collective-permute-done((f32[16,512]{1,0:T(8,128)S(1)}, f32[16,512]{1,0:T(8,128)S(1)}, u32[]{:S(2)}, u32[]{:S(2)}) %collective-permute-start.2) | collective-permute-done | bytes 32800 | tf_op jit(solution)/shard_map/ppermute | solution.py:434
  66.9 7.1 %collective-permute-start.3 = (f32[16,512]{1,0:T(8,128)S(1)}, f32[16,512]{1,0:T(8,128)S(1)}, u32[]{:S(2)}, u32[]{:S(2)}) collective-permute-start(f32[16,512]{1,0:T(8,128)S(1)} %add.20), channel_id=1, source_target_pairs={{0,128},{32,160},{64,192},{96,224},{128,0},{160,32},{192,64},{224,... | collective-permute-start | bytes 98312 | tf_op jit(solution)/shard_map/ppermute | solution.py:434
  74.0 2.4 %collective-permute-done.3 = f32[16,512]{1,0:T(8,128)S(1)} collective-permute-done((f32[16,512]{1,0:T(8,128)S(1)}, f32[16,512]{1,0:T(8,128)S(1)}, u32[]{:S(2)}, u32[]{:S(2)}) %collective-permute-start.3) | collective-permute-done | bytes 32800 | tf_op jit(solution)/shard_map/ppermute | solution.py:434
  76.4 0.1 broadcast_in_dim.4
  76.5 12.5 %all_to_all.16 = f32[16,16,512]{2,1,0:T(8,128)S(1)} all-to-all(f32[16,16,512]{2,1,0:T(8,128)S(1)} %broadcast_in_dim.4), channel_id=1, replica_groups=mesh['row'=8,'x'=4,'y'=4,'core'=2] {'x','y'}, dimensions={0} | all-to-all | bytes 1048576 | tf_op jit(solution)/shard_map/all_to_all | solution.py:436
  89.0 0.1 broadcast_in_dim.5
  89.1 4.6 %all_to_all.17.gram_ref = f32[2,16,16,512]{3,2,1,0:T(8,128)S(1)} all-to-all(f32[2,16,16,512]{3,2,1,0:T(8,128)S(1)} %broadcast_in_dim.5), channel_id=1, replica_groups=mesh['row'=8,'x'=4,'y'=4,'core'=2] {'core'}, dimensions={0} | all-to-all | bytes 2097152 | tf_op jit(solution)/shard_map/all_to_all | solution.py:437
  93.7 21.3 %inverse_factor.1.inv_ref = f32[512,512]{1,0:T(8,128)S(1)} custom-call(f32[2,16,16,512]{3,2,1,0:T(8,128)S(1)} %all_to_all.17.gram_ref), custom_call_target="tpu_custom_call" | custom-call | flops 300000000 | bytes 2097152 | tf_op jit(solution)/shard_map/inverse_factor/pallas_call | solution.py:312
  115.0 6.8 %basis_of.1 = (bf16[2,1024,512]{2,1,0:T(8,128)(2,1)S(1)}, bf16[2,1024,512]{2,1,0:T(8,128)(2,1)}, bf16[512,512]{1,0:T(8,128)(2,1)S(1)}, bf16[512,512]{1,0:T(8,128)(2,1)S(1)}) custom-call(f32[512,512]{1,0:T(8,128)S(1)} %inverse_factor.1.inv_ref, bf16[2,1024,512]{2,1,0:T(8,128)(2,1)} %get-tuple-element.28.high_ref, bf16[2,1024,512]{2,1,0:T(8,128)(2,1)} %get-tuple-element.29.low_ref), custom_call_target="tpu_custom_call" | custom-call | flops 3221225472 | bytes 8388608 | tf_op jit(solution)/shard_map/basis_of/pallas_call | solution.py:337
  121.8 12.7 %all-reduce.2.cloned.1.call-done.cross_ref = f32[512,768]{1,0:T(8,128)} async-done(((f32[512,768]{1,0:T(8,128)}), f32[512,768]{1,0:T(8,128)}) %all-reduce.2.cloned.1.call-update) | async-done | bytes 1572880 | tf_op jit(solution)/shard_map/psum | solution.py:430
  134.5 11.2 %project.1 = (f32[512,768]{1,0:T(8,128)}, f32[16,2,64,768]{3,2,1,0:T(8,128)}) custom-call(s32[1]{0:T(128)} %bitcast.core_ref, bf16[512,512]{1,0:T(8,128)(2,1)S(1)} %get-tuple-element.30.xhigh, bf16[512,512]{1,0:T(8,128)(2,1)S(1)} %get-tuple-element.31.xlow, bf16[2,1024,512]{2,1,0:T(8,128)(2,1)S(1)} %get-tuple-element.32.qhigh, ...), custom_call_target="tpu_custom_call" | custom-call | flops 4831838208 | bytes 16777216 | tf_op jit(solution)/shard_map/project/pallas_call | solution.py:379
  (3 shorter events, 0.0 us)
Async XLA Ops:
  7.2 127.3 %all-reduce.2.cloned.1.call-start = ((), (), s32[]{:S(2)}) async-start(), calls=%async_computation.3 | async-start | bytes 3145728 | tf_op jit(solution)/shard_map/psum | solution.py:430
  10.4 31.3 %copy-start = (s32[2,768]{1,0:T(2,128)S(1)}, s32[2,768]{1,0:T(2,128)}, u32[]{:S(2)}) copy-start(s32[2,768]{1,0:T(2,128)} %index_ref.1) | copy-start | bytes 18436
  41.6 5.7 %collective-permute-start = (bf16[16,64,896]{2,1,0:T(8,128)(2,1)S(1)}, bf16[16,64,896]{2,1,0:T(8,128)(2,1)S(1)}, u32[]{:S(2)}, u32[]{:S(2)}) collective-permute-start(bf16[16,64,896]{2,1,0:T(8,128)(2,1)S(1)} %all_to_all.15.refs_0_.refs_1_), channel_id=1, source_target_pairs={{0,1},{1,0},{2,3},{3,2},{4,5},{5,4},{6,7},{7,6},{8,9},{9,8},{10,11... | collective-permute-start | bytes 5505032 | tf_op jit(solution)/shard_map/ppermute | solution.py:427
  57.4 4.1 %collective-permute-start.1 = (f32[16,512]{1,0:T(8,128)S(1)}, f32[16,512]{1,0:T(8,128)S(1)}, u32[]{:S(2)}, u32[]{:S(2)}) collective-permute-start(f32[16,512]{1,0:T(8,128)S(1)} %gram_slice.1), channel_id=1, source_target_pairs={{0,32},{32,0},{64,96},{96,64},{128,160},{160,128},{192,224},{224,1... | collective-permute-start | bytes 98312 | tf_op jit(solution)/shard_map/ppermute | solution.py:434
  61.5 5.5 %collective-permute-start.2 = (f32[16,512]{1,0:T(8,128)S(1)}, f32[16,512]{1,0:T(8,128)S(1)}, u32[]{:S(2)}, u32[]{:S(2)}) collective-permute-start(f32[16,512]{1,0:T(8,128)S(1)} %add.19), channel_id=1, source_target_pairs={{0,64},{32,96},{64,0},{96,32},{128,192},{160,224},{192,128},{224,1... | collective-permute-start | bytes 98312 | tf_op jit(solution)/shard_map/ppermute | solution.py:434
  66.9 9.5 %collective-permute-start.3 = (f32[16,512]{1,0:T(8,128)S(1)}, f32[16,512]{1,0:T(8,128)S(1)}, u32[]{:S(2)}, u32[]{:S(2)}) collective-permute-start(f32[16,512]{1,0:T(8,128)S(1)} %add.20), channel_id=1, source_target_pairs={{0,128},{32,160},{64,192},{96,224},{128,0},{160,32},{192,64},{224,... | collective-permute-start | bytes 98312 | tf_op jit(solution)/shard_map/ppermute | solution.py:434
Sparse Core Ops, SparseCore 0:
  53.7 80.7 all-reduce.1

commit v4 on v3

--- a/solution.py
+++ b/solution.py
@@ -55,7 +55,8 @@
     epochs = latitude.shape[0]
     return pl.pallas_call(
         pack_kernel,
-        out_shape=jax.ShapeDtypeStruct((count, epochs, WIDE), BF16),
+        out_specs=pl.BlockSpec(memory_space=pltpu.VMEM),
+        out_shape=pltpu.VMEM((count, epochs, WIDE), BF16),
         scratch_shapes=[pltpu.VMEM((128, 128), F32)],
         compiler_params=pltpu.CompilerParams(vmem_limit_bytes=SMALL_VMEM),
         name="pack",
@@ -84,8 +85,8 @@
         table_ref, deg, order, pdeg, pord, cross_in = refs[:6]
         cross_ref, design_ref, high_ref, low_ref = refs[9:]
     else:
-        head_ref, table_ref, deg, order = refs[:4]
-        cross_ref, design_ref, high_ref, low_ref, pdeg, pord = refs[4:]
+        table_ref, deg, order = refs[:3]
+        cross_ref, design_ref, high_ref, low_ref, pdeg, pord = refs[3:]
 
     @pl.when(pl.program_id(0) == 0)
     def _():
@@ -93,7 +94,7 @@
             cross_ref[...] = cross_in[...]
             return
         cross_ref[...] = jnp.zeros_like(cross_ref)
-        head = head_ref[0].astype(F32)
+        head = table_ref[0, :, TAB:WIDE].astype(F32)
         lanes = lax.broadcasted_iota(jnp.int32, (64, NDEG), 1).astype(F32)
         wide = lax.broadcasted_iota(jnp.int32, (64, NORD), 1).astype(F32)
         for k in range(NP // 64):
@@ -103,10 +104,11 @@
             pord[64 * k : 64 * (k + 1), :] = (o == wide).astype(BF16)
 
     last = ((1,), (1,))
+    count = high_ref.shape[1] // sub
 
     def synthesize(k):
         rows = slice(k * sub, (k + 1) * sub)
-        block = slice(k * sub // 64, (k + 1) * sub // 64)
+        block = pl.ds((pl.program_id(0) * count + k) * (sub // 64), sub // 64)
 
         def columns(lo, hi):
             return table_ref[block, :, lo:hi].reshape(sub, hi - lo)
@@ -123,7 +125,6 @@
         lhs = jnp.concatenate([high.T, high.T, low.T], axis=1)
         cross_ref[...] += dot(lhs, jnp.concatenate([design[0], design[1], design[0]], axis=0))
 
-    count = high_ref.shape[1] // sub
     ready = synthesize(0)
     for k in range(count):
         following = synthesize(k + 1) if k + 1 < count else None
@@ -137,10 +138,7 @@
     half = 1 if second else 0
     whole = lambda i: (0, 0)
     along = lambda i: (half, i, 0)
-    table_spec = pl.BlockSpec((rows // 64, 64, WIDE), lambda i: (i, 0, 0))
-    fixed = [pl.BlockSpec(x.shape, whole) for x in (deg, order)]
-    panel_specs = [pl.BlockSpec((NP, NDEG), whole), pl.BlockSpec((NP, NORD), whole)]
-    cross_spec = pl.BlockSpec((NP, cols), whole)
+    here = pl.BlockSpec(memory_space=pltpu.VMEM)
     big_specs = [pl.BlockSpec((1, rows, width), along) for width in (cols, NP, NP)]
     big_shapes = [
         pltpu.HBM((2, epochs, cols), F32),
@@ -150,19 +148,19 @@
     if second:
         cross, design, high, low, pdeg, pord = prior
         args = (table, deg, order, pdeg, pord, cross, *in_hbm(design, high, low))
-        in_specs = [table_spec, *fixed, *panel_specs, cross_spec] + [pl.BlockSpec(memory_space=pl.ANY)] * 3
-        out_specs = [cross_spec, *big_specs]
+        in_specs = [here] * 6 + [pl.BlockSpec(memory_space=pl.ANY)] * 3
+        out_specs = [pl.BlockSpec((NP, cols), whole), *big_specs]
         out_shape = [pltpu.HBM((NP, cols), F32), *big_shapes]
         aliases = {6: 1, 7: 2, 8: 3}
     else:
-        args = (table, table, deg, order)
-        in_specs = [pl.BlockSpec((1, 64, 128), lambda i: (0, 0, TAB // 128)), table_spec, *fixed]
-        out_specs = [cross_spec, *big_specs, *panel_specs]
+        args = (table, deg, order)
+        in_specs = [here] * 3
+        out_specs = [here, *big_specs, here, here]
         out_shape = [
-            jax.ShapeDtypeStruct((NP, cols), F32),
+            pltpu.VMEM((NP, cols), F32),
             *big_shapes,
-            jax.ShapeDtypeStruct((NP, NDEG), BF16),
-            jax.ShapeDtypeStruct((NP, NORD), BF16),
+            pltpu.VMEM((NP, NDEG), BF16),
+            pltpu.VMEM((NP, NORD), BF16),
         ]
         aliases = {}
     return pl.pallas_call(
@@ -356,10 +354,13 @@
     @pl.when((h == 0) & (i == 0))
     def _():
         high, low = split(cross_ref[...])
-        coef = dot(xhigh[...], high) + dot(xhigh[...], low) + dot(xlow[...], high)
-        coef_ref[...] = coef
+        half = NP // 2
+        for rows, depth in ((slice(0, half), half), (slice(half, NP), NP)):
+            left = [x[rows, 0:depth] for x in (xhigh, xhigh, xlow)]
+            right = [x[0:depth] for x in (high, low, high)]
+            coef_ref[rows, :] = dot(jnp.concatenate(left, axis=1), jnp.concatenate(right, axis=0))
         put.start()
-        both[0:NP, :], both[NP : 2 * NP, :] = split(coef)
+        both[0:NP, :], both[NP : 2 * NP, :] = split(coef_ref[...])
 
     rows = design_ref.shape[1]
     high = qhigh[h, pl.ds(pl.multiple_of(i * rows, rows), rows), :]

time: 153 us -> 152 us (level)
  no operation moved by 1% of the time
where the time goes in v4:
time: 152 us
  Pallas kernels  55.6 us (37%)
  blocking collectives  50.3 us (33%)
  waiting for transfers between devices  18.9 us (12%)
  between operations  14.1 us (9%)
  starting transfers between devices  12.4 us (8%)
    all_to_all x1, blocking collectives, shards(): own = lax.all_to_all(packed, plane, 0, 0)  31.3 us
    pallas_call x1, Pallas kernels, inverse_factor(): pl.pallas_call(factor_kernel, out_shape=jax.ShapeDtypeStruct((NP, NP), F3...  21.3 us
    all_to_all x1, blocking collectives, shards(): near = lax.all_to_all(copies(summed, places), plane, 0, 0)  12.4 us
    ppermute x3, starting transfers between devices, shards(): lax.ppermute(summed, 'row', [(k, k ^ hop) for k in range(nrow)])  12.4 us
    psum x1, waiting for transfers between devices, shards(): cross = lax.psum(cross, 'row')  12.3 us
    pallas_call x2, Pallas kernels, moments(): pl.pallas_call(functools.partial(moments_kernel, second, sub), grid=(epoc...  11.5 us
    pallas_call x1, Pallas kernels, project(): pl.pallas_call(project_kernel, grid_spec=pltpu.PrefetchScalarGridSpec(num...  10.8 us
    pallas_call x1, Pallas kernels, basis_of(): pl.pallas_call(basis_kernel, grid=(halves, epochs // rows), in_specs=[who...  6.77 us
  transfers between devices with their start and end apart: 5, of which 4 were waited for; matrix products, arithmetic and copies ran while one was open for 0% of the time, Pallas kernels for 25%

profile of v4, /device:TPU:2, one launch (start us, length us, event | category | flops | bytes accessed | tf_op | source)
XLA Modules:
  0.0 151.6 jit_solution(5496234583336913563)
XLA Ops:
  7.2 0.0 all-reduce.2.cloned.1.call-start
  7.2 2.0 %all-gather.1.lead_ref = s32[2,2,768]{2,1,0:T(2,128)S(1)} all-gather(s32[1,2,768]{2,1,0:T(2,128)} %bitcast.5), channel_id=2, replica_groups=mesh['row'=8,'x'=4,'y'=4,'core'=2] {'core'}, dimensions={0}, use_global_device_ids=true | all-gather | bytes 18432 | tf_op jit(solution)/shard_map/all_gather | solution.py:424
  9.2 1.1 pack.1
  10.4 0.0 copy-start
  10.4 31.3 %all_to_all.15.refs_0_ = bf16[16,64,896]{2,1,0:T(8,128)(2,1)S(1)} all-to-all(bf16[16,64,896]{2,1,0:T(8,128)(2,1)S(1)} %pack.1), channel_id=1, replica_groups=mesh['row'=8,'x'=4,'y'=4,'core'=2] {'x','y'}, dimensions={0} | all-to-all | bytes 3670016 | tf_op jit(solution)/shard_map/all_to_all | solution.py:427
  41.6 0.0 collective-permute-start
  41.6 0.0 copy-done
  41.6 0.2 onehots.1
  41.8 5.3 %moments_first.1 = (f32[512,768]{1,0:T(8,128)S(1)}, f32[2,1024,768]{2,1,0:T(8,128)}, bf16[2,1024,512]{2,1,0:T(8,128)(2,1)}, bf16[2,1024,512]{2,1,0:T(8,128)(2,1)...) custom-call(bf16[16,64,896]{2,1,0:T(8,128)(2,1)S(1)} %all_to_all.15.refs_0_, ...), custom_call_target="tpu_custom_call" | custom-call | flops 4429185024 | bytes 7077888 | tf_op jit(solution)/shard_map/moments_first/pallas_call | solution.py:166
  47.1 0.0 collective-permute-done.refs_0_
  47.1 6.2 %moments_second.1 = (f32[512,768]{1,0:T(8,128)}, f32[2,1024,768]{2,1,0:T(8,128)}, bf16[2,1024,512]{2,1,0:T(8,128)(2,1)}, bf16[2,1024,512]{2,1,0:T(8,128)(2,1)}) custom-call(bf16[16,64,896]{2,1,0:T(8,128)(2,1)S(1)} %collective-permute-done.refs_0_, ...), custom_call_target="tpu_custom_call", output_to_operand_aliasing={{1}: (6, {}), {2}: (7, {}), {3}: (8, {})} | custom-call | flops 4429185024 | bytes 7077888 | tf_op jit(solution)/shard_map/moments_second/pallas_call | solution.py:166
  53.3 0.0 all-reduce.2.cloned.1.call-update
  53.4 3.8 %gram_slice.1 = f32[16,512]{1,0:T(8,128)S(1)} custom-call(s32[1]{0:T(128)} %bitcast.1.mine_ref, bf16[2,1024,512]{2,1,0:T(8,128)(2,1)} %get-tuple-element.28.high_ref, bf16[2,1024,512]{2,1,0:T(8,128)(2,1)} %get-tuple-element.29.low_ref), custom_call_target="tpu_custom_call" | custom-call | flops 100663296 | bytes 4194304 | tf_op jit(solution)/shard_map/gram_slice/pallas_call | solution.py:207
  57.2 2.0 %collective-permute-start.1 = (f32[16,512]{1,0:T(8,128)S(1)}, f32[16,512]{1,0:T(8,128)S(1)}, u32[]{:S(2)}, u32[]{:S(2)}) collective-permute-start(f32[16,512]{1,0:T(8,128)S(1)} %gram_slice.1), channel_id=1, source_target_pairs={{0,32},{32,0},{64,96},{96,64},{128,160},{160,128},{192,224},{224,1... | collective-permute-start | bytes 98312 | tf_op jit(solution)/shard_map/ppermute | solution.py:435
  59.3 2.0 %collective-permute-done.1 = f32[16,512]{1,0:T(8,128)S(1)} collective-permute-done((f32[16,512]{1,0:T(8,128)S(1)}, f32[16,512]{1,0:T(8,128)S(1)}, u32[]{:S(2)}, u32[]{:S(2)}) %collective-permute-start.1) | collective-permute-done | bytes 32800 | tf_op jit(solution)/shard_map/ppermute | solution.py:435
  61.3 3.3 %collective-permute-start.2 = (f32[16,512]{1,0:T(8,128)S(1)}, f32[16,512]{1,0:T(8,128)S(1)}, u32[]{:S(2)}, u32[]{:S(2)}) collective-permute-start(f32[16,512]{1,0:T(8,128)S(1)} %add.19), channel_id=1, source_target_pairs={{0,64},{32,96},{64,0},{96,32},{128,192},{160,224},{192,128},{224,1... | collective-permute-start | bytes 98312 | tf_op jit(solution)/shard_map/ppermute | solution.py:435
  64.6 2.2 %collective-permute-done.2 = f32[16,512]{1,0:T(8,128)S(1)} collective-permute-done((f32[16,512]{1,0:T(8,128)S(1)}, f32[16,512]{1,0:T(8,128)S(1)}, u32[]{:S(2)}, u32[]{:S(2)}) %collective-permute-start.2) | collective-permute-done | bytes 32800 | tf_op jit(solution)/shard_map/ppermute | solution.py:435
  66.8 7.1 %collective-permute-start.3 = (f32[16,512]{1,0:T(8,128)S(1)}, f32[16,512]{1,0:T(8,128)S(1)}, u32[]{:S(2)}, u32[]{:S(2)}) collective-permute-start(f32[16,512]{1,0:T(8,128)S(1)} %add.20), channel_id=1, source_target_pairs={{0,128},{32,160},{64,192},{96,224},{128,0},{160,32},{192,64},{224,... | collective-permute-start | bytes 98312 | tf_op jit(solution)/shard_map/ppermute | solution.py:435
  73.9 2.4 %collective-permute-done.3 = f32[16,512]{1,0:T(8,128)S(1)} collective-permute-done((f32[16,512]{1,0:T(8,128)S(1)}, f32[16,512]{1,0:T(8,128)S(1)}, u32[]{:S(2)}, u32[]{:S(2)}) %collective-permute-start.3) | collective-permute-done | bytes 32800 | tf_op jit(solution)/shard_map/ppermute | solution.py:435
  76.3 0.1 broadcast_in_dim.4
  76.4 12.4 %all_to_all.16 = f32[16,16,512]{2,1,0:T(8,128)S(1)} all-to-all(f32[16,16,512]{2,1,0:T(8,128)S(1)} %broadcast_in_dim.4), channel_id=1, replica_groups=mesh['row'=8,'x'=4,'y'=4,'core'=2] {'x','y'}, dimensions={0} | all-to-all | bytes 1048576 | tf_op jit(solution)/shard_map/all_to_all | solution.py:437
  88.8 0.1 broadcast_in_dim.5
  88.9 4.6 %all_to_all.17.gram_ref = f32[2,16,16,512]{3,2,1,0:T(8,128)S(1)} all-to-all(f32[2,16,16,512]{3,2,1,0:T(8,128)S(1)} %broadcast_in_dim.5), channel_id=1, replica_groups=mesh['row'=8,'x'=4,'y'=4,'core'=2] {'core'}, dimensions={0} | all-to-all | bytes 2097152 | tf_op jit(solution)/shard_map/all_to_all | solution.py:438
  93.5 21.3 %inverse_factor.1.inv_ref = f32[512,512]{1,0:T(8,128)S(1)} custom-call(f32[2,16,16,512]{3,2,1,0:T(8,128)S(1)} %all_to_all.17.gram_ref), custom_call_target="tpu_custom_call" | custom-call | flops 300000000 | bytes 2097152 | tf_op jit(solution)/shard_map/inverse_factor/pallas_call | solution.py:310
  114.9 6.8 %basis_of.1 = (bf16[2,1024,512]{2,1,0:T(8,128)(2,1)S(1)}, bf16[2,1024,512]{2,1,0:T(8,128)(2,1)}, bf16[512,512]{1,0:T(8,128)(2,1)S(1)}, bf16[512,512]{1,0:T(8,128)(2,1)S(1)}) custom-call(f32[512,512]{1,0:T(8,128)S(1)} %inverse_factor.1.inv_ref, bf16[2,1024,512]{2,1,0:T(8,128)(2,1)} %get-tuple-element.28.high_ref, bf16[2,1024,512]{2,1,0:T(8,128)(2,1)} %get-tuple-element.29.low_ref), custom_call_target="tpu_custom_call" | custom-call | flops 3221225472 | bytes 8388608 | tf_op jit(solution)/shard_map/basis_of/pallas_call | solution.py:335
  121.6 12.3 %all-reduce.2.cloned.1.call-done.cross_ref = f32[512,768]{1,0:T(8,128)} async-done(((f32[512,768]{1,0:T(8,128)}), f32[512,768]{1,0:T(8,128)}) %all-reduce.2.cloned.1.call-update) | async-done | bytes 1572880 | tf_op jit(solution)/shard_map/psum | solution.py:431
  133.9 10.8 %project.1 = (f32[512,768]{1,0:T(8,128)}, f32[16,2,64,768]{3,2,1,0:T(8,128)}) custom-call(s32[1]{0:T(128)} %bitcast.core_ref, bf16[512,512]{1,0:T(8,128)(2,1)S(1)} %get-tuple-element.30.xhigh, bf16[512,512]{1,0:T(8,128)(2,1)S(1)} %get-tuple-element.31.xlow, bf16[2,1024,512]{2,1,0:T(8,128)(2,1)S(1)} %get-tuple-element.32.qhigh, ...), custom_call_target="tpu_custom_call" | custom-call | flops 4831838208 | bytes 16777216 | tf_op jit(solution)/shard_map/project/pallas_call | solution.py:380
  (3 shorter events, 0.0 us)
Async XLA Ops:
  7.2 126.7 %all-reduce.2.cloned.1.call-start = ((), (), s32[]{:S(2)}) async-start(), calls=%async_computation.3 | async-start | bytes 3145728 | tf_op jit(solution)/shard_map/psum | solution.py:431
  10.4 31.3 %copy-start = (s32[2,768]{1,0:T(2,128)S(1)}, s32[2,768]{1,0:T(2,128)}, u32[]{:S(2)}) copy-start(s32[2,768]{1,0:T(2,128)} %index_ref.1) | copy-start | bytes 18436
  41.6 5.5 %collective-permute-start = (bf16[16,64,896]{2,1,0:T(8,128)(2,1)S(1)}, bf16[16,64,896]{2,1,0:T(8,128)(2,1)S(1)}, u32[]{:S(2)}, u32[]{:S(2)}) collective-permute-start(bf16[16,64,896]{2,1,0:T(8,128)(2,1)S(1)} %all_to_all.15.refs_0_), channel_id=1, source_target_pairs={{0,1},{1,0},{2,3},{3,2},{4,5},{5,4},{6,7},{7,6},{8,9},{9,8},{10,11... | collective-permute-start | bytes 5505032 | tf_op jit(solution)/shard_map/ppermute | solution.py:428
  57.2 4.1 %collective-permute-start.1 = (f32[16,512]{1,0:T(8,128)S(1)}, f32[16,512]{1,0:T(8,128)S(1)}, u32[]{:S(2)}, u32[]{:S(2)}) collective-permute-start(f32[16,512]{1,0:T(8,128)S(1)} %gram_slice.1), channel_id=1, source_target_pairs={{0,32},{32,0},{64,96},{96,64},{128,160},{160,128},{192,224},{224,1... | collective-permute-start | bytes 98312 | tf_op jit(solution)/shard_map/ppermute | solution.py:435
  61.3 5.5 %collective-permute-start.2 = (f32[16,512]{1,0:T(8,128)S(1)}, f32[16,512]{1,0:T(8,128)S(1)}, u32[]{:S(2)}, u32[]{:S(2)}) collective-permute-start(f32[16,512]{1,0:T(8,128)S(1)} %add.19), channel_id=1, source_target_pairs={{0,64},{32,96},{64,0},{96,32},{128,192},{160,224},{192,128},{224,1... | collective-permute-start | bytes 98312 | tf_op jit(solution)/shard_map/ppermute | solution.py:435
  66.8 9.5 %collective-permute-start.3 = (f32[16,512]{1,0:T(8,128)S(1)}, f32[16,512]{1,0:T(8,128)S(1)}, u32[]{:S(2)}, u32[]{:S(2)}) collective-permute-start(f32[16,512]{1,0:T(8,128)S(1)} %add.20), channel_id=1, source_target_pairs={{0,128},{32,160},{64,192},{96,224},{128,0},{160,32},{192,64},{224,... | collective-permute-start | bytes 98312 | tf_op jit(solution)/shard_map/ppermute | solution.py:435
Sparse Core Ops, SparseCore 0:
  53.5 80.3 all-reduce.1

commit v5 on v4

--- a/solution.py
+++ b/solution.py
@@ -83,10 +83,10 @@
 def moments_kernel(second, sub, *refs):
     if second:
         table_ref, deg, order, pdeg, pord, cross_in = refs[:6]
-        cross_ref, design_ref, high_ref, low_ref = refs[9:]
+        cross_ref, *big_refs, design_buf, high_buf, low_buf, sems = refs[9:]
     else:
         table_ref, deg, order = refs[:3]
-        cross_ref, design_ref, high_ref, low_ref, pdeg, pord = refs[3:]
+        cross_ref, *big_refs, pdeg, pord, design_buf, high_buf, low_buf, sems = refs[3:]
 
     @pl.when(pl.program_id(0) == 0)
     def _():
@@ -104,11 +104,18 @@
             pord[64 * k : 64 * (k + 1), :] = (o == wide).astype(BF16)
 
     last = ((1,), (1,))
-    count = high_ref.shape[1] // sub
+    count = sems.shape[0]
+
+    def writes(k):
+        rows = pl.ds(k * sub, sub)
+        return [
+            pltpu.make_async_copy(buf.at[rows, :], ref.at[int(second), rows, :], sems.at[k, n])
+            for n, (buf, ref) in enumerate(zip((design_buf, high_buf, low_buf), big_refs))
+        ]
 
     def synthesize(k):
         rows = slice(k * sub, (k + 1) * sub)
-        block = pl.ds((pl.program_id(0) * count + k) * (sub // 64), sub // 64)
+        block = slice(k * sub // 64, (k + 1) * sub // 64)
 
         def columns(lo, hi):
             return table_ref[block, :, lo:hi].reshape(sub, hi - lo)
@@ -116,9 +123,11 @@
         lat, lon = columns(0, NDEG), columns(NDEG, TAB)
         weight = columns(TAB, WIDE).astype(F32)[:, 0:1]
         high, low = split(weight * dot(lat, pdeg[...], last) * dot(lon, pord[...], last))
-        high_ref[0, rows, :], low_ref[0, rows, :] = high, low
+        high_buf[rows, :], low_buf[rows, :] = high, low
         design = weight * dot(lat, deg[...]) * dot(lon, order[...])
-        design_ref[0, rows, :] = design
+        design_buf[rows, :] = design
+        for write in writes(k):
+            write.start()
         return high, low, split(design)
 
     def accumulate(high, low, design):
@@ -130,16 +139,17 @@
         following = synthesize(k + 1) if k + 1 < count else None
         accumulate(*ready)
         ready = following
-
-
-def moments(table, deg, order, prior=None, rows=512, sub=256):
+    for k in range(count):
+        for write in writes(k):
+            write.wait()
+
+
+def moments(table, deg, order, prior=None, sub=256):
     epochs, cols = 64 * table.shape[0], deg.shape[1]
     second = prior is not None
-    half = 1 if second else 0
     whole = lambda i: (0, 0)
-    along = lambda i: (half, i, 0)
     here = pl.BlockSpec(memory_space=pltpu.VMEM)
-    big_specs = [pl.BlockSpec((1, rows, width), along) for width in (cols, NP, NP)]
+    big_specs = [pl.BlockSpec(memory_space=pl.ANY)] * 3
     big_shapes = [
         pltpu.HBM((2, epochs, cols), F32),
         pltpu.HBM((2, epochs, NP), BF16),
@@ -165,10 +175,16 @@
         aliases = {}
     return pl.pallas_call(
         functools.partial(moments_kernel, second, sub),
-        grid=(epochs // rows,),
+        grid=(1,),
         in_specs=in_specs,
         out_specs=out_specs,
         out_shape=out_shape,
+        scratch_shapes=[
+            pltpu.VMEM((epochs, cols), F32),
+            pltpu.VMEM((epochs, NP), BF16),
+            pltpu.VMEM((epochs, NP), BF16),
+            pltpu.SemaphoreType.DMA((epochs // sub, 3)),
+        ],
         input_output_aliases=aliases,
         compiler_params=pltpu.CompilerParams(vmem_limit_bytes=VMEM_LIMIT),
         cost_estimate=pl.CostEstimate(

time: 152 us -> 152 us (level)
  no operation moved by 1% of the time
where the time goes in v5:
time: 152 us
  Pallas kernels  55.6 us (37%)
  blocking collectives  50.4 us (33%)
  waiting for transfers between devices  18.9 us (12%)
  between operations  14.1 us (9%)
  starting transfers between devices  12.4 us (8%)
    all_to_all x1, blocking collectives, shards(): own = lax.all_to_all(packed, plane, 0, 0)  31.3 us
    pallas_call x1, Pallas kernels, inverse_factor(): pl.pallas_call(factor_kernel, out_shape=jax.ShapeDtypeStruct((NP, NP), F3...  21.3 us
    all_to_all x1, blocking collectives, shards(): near = lax.all_to_all(copies(summed, places), plane, 0, 0)  12.5 us
    ppermute x3, starting transfers between devices, shards(): lax.ppermute(summed, 'row', [(k, k ^ hop) for k in range(nrow)])  12.4 us
    psum x1, waiting for transfers between devices, shards(): cross = lax.psum(cross, 'row')  12.3 us
    pallas_call x2, Pallas kernels, moments(): pl.pallas_call(functools.partial(moments_kernel, second, sub), grid=(1,),...  11.5 us
    pallas_call x1, Pallas kernels, project(): pl.pallas_call(project_kernel, grid_spec=pltpu.PrefetchScalarGridSpec(num...  10.9 us
    pallas_call x1, Pallas kernels, basis_of(): pl.pallas_call(basis_kernel, grid=(halves, epochs // rows), in_specs=[who...  6.77 us
  transfers between devices with their start and end apart: 5, of which 4 were waited for; matrix products, arithmetic and copies ran while one was open for 0% of the time, Pallas kernels for 25%

profile of v5, /device:TPU:2, one launch (start us, length us, event | category | flops | bytes accessed | tf_op | source)
XLA Modules:
  0.0 151.7 jit_solution(3562260798808140987)
XLA Ops:
  7.2 0.0 all-reduce.2.cloned.1.call-start
  7.2 2.0 %all-gather.1.lead_ref = s32[2,2,768]{2,1,0:T(2,128)S(1)} all-gather(s32[1,2,768]{2,1,0:T(2,128)} %bitcast.5), channel_id=2, replica_groups=mesh['row'=8,'x'=4,'y'=4,'core'=2] {'core'}, dimensions={0}, use_global_device_ids=true | all-gather | bytes 18432 | tf_op jit(solution)/shard_map/all_gather | solution.py:440
  9.2 1.1 pack.1
  10.4 0.0 copy-start
  10.4 31.3 %all_to_all.15.refs_0_ = bf16[16,64,896]{2,1,0:T(8,128)(2,1)S(1)} all-to-all(bf16[16,64,896]{2,1,0:T(8,128)(2,1)S(1)} %pack.1), channel_id=1, replica_groups=mesh['row'=8,'x'=4,'y'=4,'core'=2] {'x','y'}, dimensions={0} | all-to-all | bytes 3670016 | tf_op jit(solution)/shard_map/all_to_all | solution.py:443
  41.6 0.0 collective-permute-start
  41.6 0.0 copy-done
  41.6 0.2 onehots.1
  41.8 5.3 %moments_first.1 = (f32[512,768]{1,0:T(8,128)S(1)}, f32[2,1024,768]{2,1,0:T(8,128)}, bf16[2,1024,512]{2,1,0:T(8,128)(2,1)}, bf16[2,1024,512]{2,1,0:T(8,128)(2,1)...) custom-call(bf16[16,64,896]{2,1,0:T(8,128)(2,1)S(1)} %all_to_all.15.refs_0_, ...), custom_call_target="tpu_custom_call" | custom-call | flops 4429185024 | bytes 7077888 | tf_op jit(solution)/shard_map/moments_first/pallas_call | solution.py:176
  47.1 0.0 collective-permute-done.refs_0_
  47.1 6.2 %moments_second.1 = (f32[512,768]{1,0:T(8,128)}, f32[2,1024,768]{2,1,0:T(8,128)}, bf16[2,1024,512]{2,1,0:T(8,128)(2,1)}, bf16[2,1024,512]{2,1,0:T(8,128)(2,1)}) custom-call(bf16[16,64,896]{2,1,0:T(8,128)(2,1)S(1)} %collective-permute-done.refs_0_, ...), custom_call_target="tpu_custom_call", output_to_operand_aliasing={{1}: (6, {}), {2}: (7, {}), {3}: (8, {})} | custom-call | flops 4429185024 | bytes 7077888 | tf_op jit(solution)/shard_map/moments_second/pallas_call | solution.py:176
  53.4 0.0 all-reduce.2.cloned.1.call-update
  53.4 3.8 %gram_slice.1 = f32[16,512]{1,0:T(8,128)S(1)} custom-call(s32[1]{0:T(128)} %bitcast.1.mine_ref, bf16[2,1024,512]{2,1,0:T(8,128)(2,1)} %get-tuple-element.28.high_ref, bf16[2,1024,512]{2,1,0:T(8,128)(2,1)} %get-tuple-element.29.low_ref), custom_call_target="tpu_custom_call" | custom-call | flops 100663296 | bytes 4194304 | tf_op jit(solution)/shard_map/gram_slice/pallas_call | solution.py:223
  57.3 2.0 %collective-permute-start.1 = (f32[16,512]{1,0:T(8,128)S(1)}, f32[16,512]{1,0:T(8,128)S(1)}, u32[]{:S(2)}, u32[]{:S(2)}) collective-permute-start(f32[16,512]{1,0:T(8,128)S(1)} %gram_slice.1), channel_id=1, source_target_pairs={{0,32},{32,0},{64,96},{96,64},{128,160},{160,128},{192,224},{224,1... | collective-permute-start | bytes 98312 | tf_op jit(solution)/shard_map/ppermute | solution.py:451
  59.3 2.1 %collective-permute-done.1 = f32[16,512]{1,0:T(8,128)S(1)} collective-permute-done((f32[16,512]{1,0:T(8,128)S(1)}, f32[16,512]{1,0:T(8,128)S(1)}, u32[]{:S(2)}, u32[]{:S(2)}) %collective-permute-start.1) | collective-permute-done | bytes 32800 | tf_op jit(solution)/shard_map/ppermute | solution.py:451
  61.3 3.3 %collective-permute-start.2 = (f32[16,512]{1,0:T(8,128)S(1)}, f32[16,512]{1,0:T(8,128)S(1)}, u32[]{:S(2)}, u32[]{:S(2)}) collective-permute-start(f32[16,512]{1,0:T(8,128)S(1)} %add.19), channel_id=1, source_target_pairs={{0,64},{32,96},{64,0},{96,32},{128,192},{160,224},{192,128},{224,1... | collective-permute-start | bytes 98312 | tf_op jit(solution)/shard_map/ppermute | solution.py:451
  64.6 2.2 %collective-permute-done.2 = f32[16,512]{1,0:T(8,128)S(1)} collective-permute-done((f32[16,512]{1,0:T(8,128)S(1)}, f32[16,512]{1,0:T(8,128)S(1)}, u32[]{:S(2)}, u32[]{:S(2)}) %collective-permute-start.2) | collective-permute-done | bytes 32800 | tf_op jit(solution)/shard_map/ppermute | solution.py:451
  66.8 7.1 %collective-permute-start.3 = (f32[16,512]{1,0:T(8,128)S(1)}, f32[16,512]{1,0:T(8,128)S(1)}, u32[]{:S(2)}, u32[]{:S(2)}) collective-permute-start(f32[16,512]{1,0:T(8,128)S(1)} %add.20), channel_id=1, source_target_pairs={{0,128},{32,160},{64,192},{96,224},{128,0},{160,32},{192,64},{224,... | collective-permute-start | bytes 98312 | tf_op jit(solution)/shard_map/ppermute | solution.py:451
  73.9 2.4 %collective-permute-done.3 = f32[16,512]{1,0:T(8,128)S(1)} collective-permute-done((f32[16,512]{1,0:T(8,128)S(1)}, f32[16,512]{1,0:T(8,128)S(1)}, u32[]{:S(2)}, u32[]{:S(2)}) %collective-permute-start.3) | collective-permute-done | bytes 32800 | tf_op jit(solution)/shard_map/ppermute | solution.py:451
  76.3 0.1 broadcast_in_dim.4
  76.3 12.5 %all_to_all.16 = f32[16,16,512]{2,1,0:T(8,128)S(1)} all-to-all(f32[16,16,512]{2,1,0:T(8,128)S(1)} %broadcast_in_dim.4), channel_id=1, replica_groups=mesh['row'=8,'x'=4,'y'=4,'core'=2] {'x','y'}, dimensions={0} | all-to-all | bytes 1048576 | tf_op jit(solution)/shard_map/all_to_all | solution.py:453
  88.8 0.1 broadcast_in_dim.5
  89.0 4.6 %all_to_all.17.gram_ref = f32[2,16,16,512]{3,2,1,0:T(8,128)S(1)} all-to-all(f32[2,16,16,512]{3,2,1,0:T(8,128)S(1)} %broadcast_in_dim.5), channel_id=1, replica_groups=mesh['row'=8,'x'=4,'y'=4,'core'=2] {'core'}, dimensions={0} | all-to-all | bytes 2097152 | tf_op jit(solution)/shard_map/all_to_all | solution.py:454
  93.5 21.3 %inverse_factor.1.inv_ref = f32[512,512]{1,0:T(8,128)S(1)} custom-call(f32[2,16,16,512]{3,2,1,0:T(8,128)S(1)} %all_to_all.17.gram_ref), custom_call_target="tpu_custom_call" | custom-call | flops 300000000 | bytes 2097152 | tf_op jit(solution)/shard_map/inverse_factor/pallas_call | solution.py:326
  114.9 6.8 %basis_of.1 = (bf16[2,1024,512]{2,1,0:T(8,128)(2,1)S(1)}, bf16[2,1024,512]{2,1,0:T(8,128)(2,1)}, bf16[512,512]{1,0:T(8,128)(2,1)S(1)}, bf16[512,512]{1,0:T(8,128)(2,1)S(1)}) custom-call(f32[512,512]{1,0:T(8,128)S(1)} %inverse_factor.1.inv_ref, bf16[2,1024,512]{2,1,0:T(8,128)(2,1)} %get-tuple-element.28.high_ref, bf16[2,1024,512]{2,1,0:T(8,128)(2,1)} %get-tuple-element.29.low_ref), custom_call_target="tpu_custom_call" | custom-call | flops 3221225472 | bytes 8388608 | tf_op jit(solution)/shard_map/basis_of/pallas_call | solution.py:351
  121.7 12.3 %all-reduce.2.cloned.1.call-done.cross_ref = f32[512,768]{1,0:T(8,128)} async-done(((f32[512,768]{1,0:T(8,128)}), f32[512,768]{1,0:T(8,128)}) %all-reduce.2.cloned.1.call-update) | async-done | bytes 1572880 | tf_op jit(solution)/shard_map/psum | solution.py:447
  134.0 10.9 %project.1 = (f32[512,768]{1,0:T(8,128)}, f32[16,2,64,768]{3,2,1,0:T(8,128)}) custom-call(s32[1]{0:T(128)} %bitcast.core_ref, bf16[512,512]{1,0:T(8,128)(2,1)S(1)} %get-tuple-element.30.xhigh, bf16[512,512]{1,0:T(8,128)(2,1)S(1)} %get-tuple-element.31.xlow, bf16[2,1024,512]{2,1,0:T(8,128)(2,1)S(1)} %get-tuple-element.32.qhigh, ...), custom_call_target="tpu_custom_call" | custom-call | flops 4831838208 | bytes 16777216 | tf_op jit(solution)/shard_map/project/pallas_call | solution.py:396
  (3 shorter events, 0.0 us)
Async XLA Ops:
  7.2 126.8 %all-reduce.2.cloned.1.call-start = ((), (), s32[]{:S(2)}) async-start(), calls=%async_computation.3 | async-start | bytes 3145728 | tf_op jit(solution)/shard_map/psum | solution.py:447
  10.4 31.3 %copy-start = (s32[2,768]{1,0:T(2,128)S(1)}, s32[2,768]{1,0:T(2,128)}, u32[]{:S(2)}) copy-start(s32[2,768]{1,0:T(2,128)} %index_ref.1) | copy-start | bytes 18436
  41.6 5.5 %collective-permute-start = (bf16[16,64,896]{2,1,0:T(8,128)(2,1)S(1)}, bf16[16,64,896]{2,1,0:T(8,128)(2,1)S(1)}, u32[]{:S(2)}, u32[]{:S(2)}) collective-permute-start(bf16[16,64,896]{2,1,0:T(8,128)(2,1)S(1)} %all_to_all.15.refs_0_), channel_id=1, source_target_pairs={{0,1},{1,0},{2,3},{3,2},{4,5},{5,4},{6,7},{7,6},{8,9},{9,8},{10,11... | collective-permute-start | bytes 5505032 | tf_op jit(solution)/shard_map/ppermute | solution.py:444
  57.3 4.1 %collective-permute-start.1 = (f32[16,512]{1,0:T(8,128)S(1)}, f32[16,512]{1,0:T(8,128)S(1)}, u32[]{:S(2)}, u32[]{:S(2)}) collective-permute-start(f32[16,512]{1,0:T(8,128)S(1)} %gram_slice.1), channel_id=1, source_target_pairs={{0,32},{32,0},{64,96},{96,64},{128,160},{160,128},{192,224},{224,1... | collective-permute-start | bytes 98312 | tf_op jit(solution)/shard_map/ppermute | solution.py:451
  61.3 5.5 %collective-permute-start.2 = (f32[16,512]{1,0:T(8,128)S(1)}, f32[16,512]{1,0:T(8,128)S(1)}, u32[]{:S(2)}, u32[]{:S(2)}) collective-permute-start(f32[16,512]{1,0:T(8,128)S(1)} %add.19), channel_id=1, source_target_pairs={{0,64},{32,96},{64,0},{96,32},{128,192},{160,224},{192,128},{224,1... | collective-permute-start | bytes 98312 | tf_op jit(solution)/shard_map/ppermute | solution.py:451
  66.8 9.5 %collective-permute-start.3 = (f32[16,512]{1,0:T(8,128)S(1)}, f32[16,512]{1,0:T(8,128)S(1)}, u32[]{:S(2)}, u32[]{:S(2)}) collective-permute-start(f32[16,512]{1,0:T(8,128)S(1)} %add.20), channel_id=1, source_target_pairs={{0,128},{32,160},{64,192},{96,224},{128,0},{160,32},{192,64},{224,... | collective-permute-start | bytes 98312 | tf_op jit(solution)/shard_map/ppermute | solution.py:451
Sparse Core Ops, SparseCore 0:
  53.5 80.3 all-reduce.1
